TPU v7x, 256 devices: a whole 4x4x8 slice. The times are simulated.
256 devices in a mesh: gx: 16 (over z_hi, x), gy: 16 (over y, z_lo, core).
Axes of the slice: x: 4, y: 4, z: 8 (z_hi: 4, z_lo: 2; z = z_hi * 2 + z_lo), core: 2. Of those that a mesh axis runs over, the one named last changes fastest.
Arguments:
- positions: float32 [3, 32768], P(None, ('gx', 'gy')), may hold values from -1 to 512, as said below
- features: bfloat16 [64, 32768], P(None, ('gx', 'gy')), may hold values from -6 to 6
- species: int32 [32768], P(('gx', 'gy')), may hold values from 0 to 4
- edge_list: int32 [2, 917504], P(None, ('gx', 'gy')), may hold values from 0 to 319, as said below
- edge_count: int32 [256], P(('gx', 'gy')), may hold values from 1 to 3136, as said below
- send_list_x: int32 [32768], P(('gx', 'gy')), may hold values from 0 to 127, as said below
- send_list_y: int32 [16384], P(('gx', 'gy')), may hold values from 0 to 255, as said below
- radial_in: float32 [64, 8], replicated, may hold values from -12 to 12
- radial_out: float32 [192, 64], replicated, may hold values from -0.75 to 0.75
- mix_weight: float32 [64, 192], replicated, may hold values from -0.4375 to 0.4375
- out_weight: float32 [64], replicated, may hold values from -0.75 to 0.75
- species_energy: float32 [5], replicated, may hold values from -6 to 6
Outputs:
- energies: float32 [32768], P(('gx', 'gy'))
- forces: float32 [3, 32768], P(None, ('gx', 'gy'))
Inputs may be any that keep to these rules, and one draw needn't show every extreme that they name: `positions`: atoms sit on a lattice of cells with random displacements; each device holds the cells of its column in a random slot order. Each pair of lattice neighbours within 2 cells is listed at most once in all, on the device of its first atom, and only if both atoms exist; its second entry never names a copy that no device sends. `edge_list`: row 0 names own slots below 128, row 1 entries of the extended list; slots from edge_count on hold zeros. `edge_count`: every device has at most 3136 live pairs, and some device has exactly 3136 in every draw; counts differ widely between devices. `send_list_x`: each half names 64 distinct own slots. `send_list_y`: each half names 32 distinct entries among own atoms and x copies.
All inputs are finite; a program needn't handle non-finite values.
Results may differ from a plain program's by a relative error of at most 0.00055.
Values sent between devices are 32-bit elements; how exact they have to be, the bound alone decides.
A program may use at most 64 MiB of HBM per device.

v0:
```python
import math

import jax
import jax.numpy as jnp
import numpy as np
from jax import lax
from jax.sharding import PartitionSpec as P

EDGE_BLOCK = 512


cutoff_radius = 5.0
message_scale = 0.3
degree_of = np.array([0, 1, 1, 1, 2, 2, 2, 2, 2], np.int32)
parity_sign = np.array([1.0, -1.0, -1.0, -1.0, 1.0, 1.0, 1.0, 1.0, 1.0], np.float32)
highest = lax.Precision.HIGHEST


def padded(block, sides, width):
    for axis, dim in sides:
        count = lax.axis_size(axis)
        forward = [(i, i + 1) for i in range(count - 1)]
        backward = [(target, source) for source, target in forward]
        low = lax.ppermute(
            lax.slice_in_dim(block, block.shape[dim] - width, None, axis=dim), axis, forward
        )
        high = lax.ppermute(lax.slice_in_dim(block, 0, width, axis=dim), axis, backward)
        block = jnp.concatenate([low, block, high], axis=dim)
    return block


def harmonics(direction):
    along_x, along_y, along_z = (direction[0], direction[1], direction[2])
    root_three = math.sqrt(3.0)
    root_five = math.sqrt(5.0)
    root_fifteen = math.sqrt(15.0)
    return jnp.stack(
        [
            jnp.ones_like(along_x),
            root_three * along_x,
            root_three * along_y,
            root_three * along_z,
            root_fifteen * along_x * along_y,
            root_fifteen * along_y * along_z,
            0.5 * root_five * (3.0 * along_z * along_z - 1.0),
            root_fifteen * along_x * along_z,
            0.5 * root_fifteen * (along_x * along_x - along_y * along_y),
        ]
    )


def edge_messages(relative, live_mask, own_features, other_features, radial_in, radial_out):
    distance = jnp.sqrt(jnp.sum(relative * relative, axis=0))
    direction = relative / distance
    orders = jnp.arange(1, radial_in.shape[1] + 1, dtype=jnp.float32)[:, None]
    bessel = (
        math.sqrt(2.0 / cutoff_radius)
        * jnp.sin(orders * (math.pi / cutoff_radius) * distance)
        / distance
    )
    scaled = distance / cutoff_radius
    envelope = jnp.where(distance < cutoff_radius, (1.0 - scaled * scaled) ** 2, 0.0)
    hidden = jax.nn.silu(jnp.dot(radial_in, bessel, precision=highest))
    radial = jnp.dot(radial_out, hidden, precision=highest) * (envelope * live_mask)
    channels = own_features.shape[0]
    edge_total = distance.shape[0]
    radial = radial.reshape(3, channels, edge_total)[degree_of]
    shapes = harmonics(direction) * message_scale
    toward_own = shapes[:, None, :] * radial * other_features[None]
    toward_other = (shapes * parity_sign[:, None])[:, None, :] * radial * own_features[None]
    return (
        toward_own.reshape(9 * channels, edge_total),
        toward_other.reshape(9 * channels, edge_total),
    )


def atom_energy(partial_value, feature_rows, mix_weight, out_weight):
    channels = feature_rows.shape[0]
    cube = partial_value.reshape(9, channels, -1)
    square = cube * cube
    invariant = jnp.concatenate(
        [square[0], jnp.sum(square[1:4], axis=0), jnp.sum(square[4:9], axis=0)], axis=0
    )
    mixed = jnp.dot(mix_weight, invariant, precision=highest) + feature_rows
    return jnp.dot(out_weight, jax.nn.silu(mixed), precision=highest)


def species_shift(species, species_energy):
    kinds = jnp.arange(species_energy.shape[0], dtype=jnp.int32)
    onehot = (species[None, :] == kinds[:, None]).astype(jnp.float32)
    return jnp.dot(species_energy, onehot, precision=highest)


def spread(rows_data, send_list_x, send_list_y):
    ghost_x = send_list_x.shape[0] // 2
    ghost_y = send_list_y.shape[0] // 2
    outgoing = jnp.take(rows_data, send_list_x, axis=1)
    arrived = padded(outgoing, (("gx", 1),), ghost_x)
    section_one = jnp.concatenate(
        [rows_data, arrived[:, :ghost_x], arrived[:, 3 * ghost_x :]], axis=1
    )
    outgoing = jnp.take(section_one, send_list_y, axis=1)
    arrived = padded(outgoing, (("gy", 1),), ghost_y)
    return jnp.concatenate([section_one, arrived[:, :ghost_y], arrived[:, 3 * ghost_y :]], axis=1)


def collect(extended, atoms_here, send_list_x, send_list_y):
    ghost_x = send_list_x.shape[0] // 2
    ghost_y = send_list_y.shape[0] // 2
    width_one = atoms_here + 2 * ghost_x
    returned = padded(extended[:, width_one:], (("gy", 1),), ghost_y)
    incoming = jnp.concatenate([returned[:, :ghost_y], returned[:, 3 * ghost_y :]], axis=1)
    section_one = extended[:, :width_one].at[:, send_list_y].add(incoming)
    returned = padded(section_one[:, atoms_here:], (("gx", 1),), ghost_x)
    incoming = jnp.concatenate([returned[:, :ghost_x], returned[:, 3 * ghost_x :]], axis=1)
    return section_one[:, :atoms_here].at[:, send_list_x].add(incoming)


def pick_rows(rows_data, table):
    return lax.dot_general(
        rows_data,
        table,
        (((1,), (0,)), ((), ())),
        precision=highest,
        preferred_element_type=jnp.float32,
    )


def place_rows(values, table):
    return lax.dot_general(
        values,
        table,
        (((1,), (1,)), ((), ())),
        precision=highest,
        preferred_element_type=jnp.float32,
    )


def edge_block(edge_list, offset, live_total, extended, atoms_here):
    pair_rows = lax.dynamic_slice_in_dim(edge_list, offset, EDGE_BLOCK, 1)
    first_row, second_row = (pair_rows[0], pair_rows[1])
    live_row = offset + jnp.arange(EDGE_BLOCK, dtype=jnp.int32) < live_total
    first_table = (jnp.arange(atoms_here, dtype=jnp.int32)[:, None] == first_row[None, :]).astype(
        jnp.float32
    )
    second_table = (
        jnp.arange(extended.shape[1], dtype=jnp.int32)[:, None] == second_row[None, :]
    ).astype(jnp.float32)
    first_data = pick_rows(extended[:, :atoms_here], first_table)
    second_data = pick_rows(extended, second_table)
    relative = second_data[:3] - first_data[:3]
    filler = jnp.array([[2.0], [0.0], [0.0]], jnp.float32)
    relative = jnp.where(live_row[None, :], relative, filler)
    return (
        first_table,
        second_table,
        live_row.astype(jnp.float32),
        relative,
        first_data[3:],
        second_data[3:],
    )


def local(
    positions,
    features,
    species,
    edge_list,
    edge_count,
    send_list_x,
    send_list_y,
    radial_in,
    radial_out,
    mix_weight,
    out_weight,
    species_energy,
):
    atoms_here = positions.shape[1]
    channels = features.shape[0]
    own_features = features.astype(jnp.float32)
    extended = spread(jnp.concatenate([positions, own_features], axis=0), send_list_x, send_list_y)
    live_total = edge_count[0]
    block_total = edge_list.shape[1] // EDGE_BLOCK

    def forward_step(block_number, partial_value):
        first_table, second_table, live_mask, relative, first_features, second_features = (
            edge_block(edge_list, block_number * EDGE_BLOCK, live_total, extended, atoms_here)
        )
        toward_first, toward_second = edge_messages(
            relative, live_mask, first_features, second_features, radial_in, radial_out
        )
        partial_value = partial_value + place_rows(toward_second, second_table)
        return partial_value.at[:, :atoms_here].add(place_rows(toward_first, first_table))

    empty_sums = jnp.zeros((9 * channels, extended.shape[1]), jnp.float32)
    partial_value = lax.fori_loop(0, block_total, forward_step, empty_sums)
    own_sums = collect(partial_value, atoms_here, send_list_x, send_list_y)

    def readout_own(sums_in):
        return atom_energy(sums_in, own_features, mix_weight, out_weight)

    energy_own, pullback = jax.vjp(readout_own, own_sums)
    (own_gradient,) = pullback(jnp.ones_like(energy_own))
    extended_gradient = spread(own_gradient, send_list_x, send_list_y)

    def backward_step(block_number, force_rows):
        first_table, second_table, live_mask, relative, first_features, second_features = (
            edge_block(edge_list, block_number * EDGE_BLOCK, live_total, extended, atoms_here)
        )

        def messages_of(relative_in):
            return edge_messages(
                relative_in, live_mask, first_features, second_features, radial_in, radial_out
            )

        ignored, pullback_edges = jax.vjp(messages_of, relative)
        first_gradient = pick_rows(extended_gradient[:, :atoms_here], first_table)
        second_gradient = pick_rows(extended_gradient, second_table)
        (pulled,) = pullback_edges((first_gradient, second_gradient))
        force_rows = force_rows - place_rows(pulled, second_table)
        return force_rows.at[:, :atoms_here].add(place_rows(pulled, first_table))

    empty_forces = jnp.zeros((3, extended.shape[1]), jnp.float32)
    force_rows = lax.fori_loop(0, block_total, backward_step, empty_forces)
    forces = collect(force_rows, atoms_here, send_list_x, send_list_y)
    energies = energy_own + species_shift(species, species_energy)
    return (energies, forces)


def solution(mesh):
    placed = (
        P(None, ("gx", "gy")),
        P(None, ("gx", "gy")),
        P(("gx", "gy")),
        P(None, ("gx", "gy")),
        P(("gx", "gy")),
        P(("gx", "gy")),
        P(("gx", "gy")),
        P(),
        P(),
        P(),
        P(),
        P(),
    )
    return jax.shard_map(
        local,
        mesh=mesh,
        in_specs=placed,
        out_specs=(P(("gx", "gy")), P(None, ("gx", "gy"))),
        check_vma=False,
    )
```

profile of v0, /device:TPU:136, one launch (start us, length us, event | category | flops | bytes accessed | tf_op | source)
XLA Modules:
  0.0 368.4 jit_solution(1751813024959678089)
XLA Ops:
  4.4 3.4 collective-permute-start
  7.8 6.7 %collective-permute-start.1 = (f32[67,64]{1,0:T(8,128)S(1)}, f32[67,64]{1,0:T(8,128)S(1)}, u32[]{:S(2)}, u32[]{:S(2)}) collective-permute-start(f32[67,64]{1,0:T(8,128)S(1)} %get-tuple-element.841), channel_id=1, source_target_pairs={{16,0},{32,16},{48,32},{64,48},{80,64},{96,80},{112,96},{128,112},... | collective-permute-start | bytes 51464 | tf_op jit(solution)/shard_map/ppermute | solution.py:27
  17.8 1.9 collective-permute-start.2
  19.7 4.5 %collective-permute-start.3 = (f32[67,32]{1,0:T(8,128)S(1)}, f32[67,32]{1,0:T(8,128)S(1)}, u32[]{:S(2)}, u32[]{:S(2)}) collective-permute-start(f32[67,32]{1,0:T(8,128)S(1)} %get-tuple-element.839), channel_id=1, source_target_pairs={{1,0},{2,1},{3,2},{4,3},{5,4},{6,5},{7,6},{8,7},{9,8},{10,9},{11,1... | collective-permute-start | bytes 25736 | tf_op jit(solution)/shard_map/ppermute | solution.py:27
  24.2 1.6 collective-permute-done.3
  26.1 69.1 %while.34 = (s32[]{:T(128)}, f32[576,320]{0,1:T(8,128)S(1)}, s32[]{:T(128)}, s32[2,3584]{1,0:T(2,128)}, f32[67,320]{1,0:T(8,128)S(1)}, /*index=5*/f32[67,128]{1,...) while((s32[]{:T(128)}, f32[576,320]{0,1:T(8,128)S(1)}, ...), condition=%wide.region_3.4_spmd.clone, body=%wide.region_0.3_spmd.sunk.clone.sunk | while | flops 1850754560 | bytes 12496065 | solution.py:196
  34.5 1.4 fusion.174
  44.4 1.4 fusion.174
  54.2 1.4 fusion.174
  64.1 1.4 fusion.174
  74.0 1.4 fusion.174
  83.8 1.4 fusion.174
  93.7 1.4 fusion.174
  95.2 4.6 %collective-permute-start.5 = (f32[576,32]{0,1:T(8,128)S(1)}, f32[576,32]{0,1:T(8,128)S(1)}, u32[]{:S(2)}, u32[]{:S(2)}) collective-permute-start(f32[576,32]{0,1:T(8,128)S(1)} %get-tuple-element.827), channel_id=1, source_target_pairs={{1,0},{2,1},{3,2},{4,3},{5,4},{6,5},{7,6},{8,7},{9,8},{10,9},{11,1... | collective-permute-start | bytes 221192 | tf_op jit(solution)/shard_map/ppermute | solution.py:27
  99.7 1.9 collective-permute-start.4
  102.0 4.4 %collective-permute-done.4 = f32[576,32]{0,1:T(8,128)S(1)} collective-permute-done((f32[576,32]{0,1:T(8,128)S(1)}, f32[576,32]{0,1:T(8,128)S(1)}, u32[]{:S(2)}, u32[]{:S(2)}) %collective-permute-start.4) | collective-permute-done | bytes 73760 | tf_op jit(solution)/shard_map/ppermute | solution.py:24
  107.7 8.4 %collective-permute-start.7 = (f32[576,64]{0,1:T(8,128)S(1)}, f32[576,64]{0,1:T(8,128)S(1)}, u32[]{:S(2)}, u32[]{:S(2)}) collective-permute-start(f32[576,64]{0,1:T(8,128)S(1)} %get-tuple-element.829), channel_id=1, source_target_pairs={{16,0},{32,16},{48,32},{64,48},{80,64},{96,80},{112,96},{128,112},... | collective-permute-start | bytes 442376 | tf_op jit(solution)/shard_map/ppermute | solution.py:27
  116.2 1.9 collective-permute-start.6
  119.4 8.3 %collective-permute-done.6 = f32[576,64]{0,1:T(8,128)S(1)} collective-permute-done((f32[576,64]{0,1:T(8,128)S(1)}, f32[576,64]{0,1:T(8,128)S(1)}, u32[]{:S(2)}, u32[]{:S(2)}) %collective-permute-start.6) | collective-permute-done | bytes 147488 | tf_op jit(solution)/shard_map/ppermute | solution.py:24
  127.7 1.6 scatter_custom_fusion.2
  132.6 1.9 collective-permute-start.8
  134.5 8.1 %collective-permute-start.9 = (f32[576,64]{0,1:T(8,128)S(1)}, f32[576,64]{0,1:T(8,128)S(1)}, u32[]{:S(2)}, u32[]{:S(2)}) collective-permute-start(f32[576,64]{0,1:T(8,128)S(1)} %get-tuple-element.830), channel_id=1, source_target_pairs={{16,0},{32,16},{48,32},{64,48},{80,64},{96,80},{112,96},{128,112},... | collective-permute-start | bytes 442376 | tf_op jit(solution)/shard_map/ppermute | solution.py:27
  142.7 1.5 collective-permute-done.8
  144.1 4.9 %collective-permute-done.9 = f32[576,64]{0,1:T(8,128)S(1)} collective-permute-done((f32[576,64]{0,1:T(8,128)S(1)}, f32[576,64]{0,1:T(8,128)S(1)}, u32[]{:S(2)}, u32[]{:S(2)}) %collective-permute-start.9) | collective-permute-done | bytes 147488 | tf_op jit(solution)/shard_map/ppermute | solution.py:27
  150.0 1.9 collective-permute-start.10
  151.9 4.7 %collective-permute-start.11 = (f32[576,32]{0,1:T(8,128)S(1)}, f32[576,32]{0,1:T(8,128)S(1)}, u32[]{:S(2)}, u32[]{:S(2)}) collective-permute-start(f32[576,32]{0,1:T(8,128)S(1)} %get-tuple-element.832), channel_id=1, source_target_pairs={{1,0},{2,1},{3,2},{4,3},{5,4},{6,5},{7,6},{8,7},{9,8},{10,9},{11,1... | collective-permute-start | bytes 221192 | tf_op jit(solution)/shard_map/ppermute | solution.py:27
  157.1 1.4 collective-permute-done.11
  160.5 174.4 %while.35 = (s32[]{:T(128)}, f32[3,320]{1,0:T(4,128)}, s32[]{:T(128)}, s32[2,3584]{1,0:T(2,128)}, f32[67,320]{1,0:T(8,128)S(1)}, /*index=5*/f32[67,128]{1,0:T(8,...) while((s32[]{:T(128)}, f32[3,320]{1,0:T(4,128)}, ...), condition=%wide.region_18.19_spmd.clone, body=%wide.region_8.18_spmd.sunk.clone.sunk | while | flops 1940001536 | bytes 21319116 | solution.py:224
  168.5 2.3 fusion.188
  171.5 1.7 fusion.189
  174.7 2.8 multiply_reduce_fusion.11
  177.7 2.9 scatter_fusion
  193.4 2.3 fusion.188
  196.4 1.7 fusion.189
  199.6 2.8 multiply_reduce_fusion.11
  202.6 2.9 scatter_fusion
  218.3 2.3 fusion.188
  221.3 1.7 fusion.189
  224.5 2.8 multiply_reduce_fusion.11
  227.5 2.9 scatter_fusion
  243.2 2.3 fusion.188
  246.3 1.7 fusion.189
  249.4 2.8 multiply_reduce_fusion.11
  252.4 2.9 scatter_fusion
  268.1 2.3 fusion.188
  271.2 1.7 fusion.189
  274.3 2.8 multiply_reduce_fusion.11
  277.3 2.9 scatter_fusion
  293.0 2.3 fusion.188
  296.1 1.7 fusion.189
  299.2 2.8 multiply_reduce_fusion.11
  302.2 2.9 scatter_fusion
  318.0 2.3 fusion.188
  321.0 1.7 fusion.189
  324.1 2.8 multiply_reduce_fusion.11
  327.2 2.9 scatter_fusion
  335.7 4.6 %collective-permute-start.13 = (f32[3,32]{1,0:T(4,128)S(1)}, f32[3,32]{1,0:T(4,128)S(1)}, u32[]{:S(2)}, u32[]{:S(2)}) collective-permute-start(f32[3,32]{1,0:T(4,128)S(1)} %get-tuple-element.844), channel_id=1, source_target_pairs={{1,0},{2,1},{3,2},{4,3},{5,4},{6,5},{7,6},{8,7},{9,8},{10,9},{11,1... | collective-permute-start | bytes 1160 | tf_op jit(solution)/shard_map/ppermute | solution.py:27
  340.3 1.9 collective-permute-start.12
  343.8 2.2 collective-permute-done.12
  347.4 8.7 %collective-permute-start.15 = (f32[3,64]{0,1:T(8,128)S(1)}, f32[3,64]{0,1:T(8,128)S(1)}, u32[]{:S(2)}, u32[]{:S(2)}) collective-permute-start(f32[3,64]{0,1:T(8,128)S(1)} %get-tuple-element.835), channel_id=1, source_target_pairs={{16,0},{32,16},{48,32},{64,48},{80,64},{96,80},{112,96},{128,112},... | collective-permute-start | bytes 2312 | tf_op jit(solution)/shard_map/ppermute | solution.py:27
  356.1 1.9 collective-permute-start.14
  358.0 1.4 fusion.74
  359.5 6.6 %collective-permute-done.14 = f32[3,64]{0,1:T(8,128)S(1)} collective-permute-done((f32[3,64]{0,1:T(8,128)S(1)}, f32[3,64]{0,1:T(8,128)S(1)}, u32[]{:S(2)}, u32[]{:S(2)}) %collective-permute-start.14) | collective-permute-done | bytes 800 | tf_op jit(solution)/shard_map/ppermute | solution.py:24
  366.4 1.4 scatter_fusion.2
  (856 shorter events, 182.8 us)
Async XLA Ops:
  0.6 129.5 %copy-start = (f32[64,192]{1,0:T(8,128)S(1)}, f32[64,192]{1,0:T(8,128)}, u32[]{:S(2)}) copy-start(f32[64,192]{1,0:T(8,128)} %param.36) | copy-start | bytes 147460
  1.3 126.4 %copy-start.39 = (s32[128]{0:T(128)}, s32[128]{0:T(128)S(1)}, u32[]{:S(2)}) copy-start(s32[128]{0:T(128)S(1)} %compare_select_fusion.1) | copy-start | bytes 1540
  4.3 21.7 %copy-start.4 = (f32[192,64]{0,1:T(8,128)S(1)}, f32[192,64]{0,1:T(8,128)}, u32[]{:S(2)}) copy-start(f32[192,64]{0,1:T(8,128)} %param.35) | copy-start | bytes 147460
  4.3 21.7 %copy-start.21 = (f32[64,8]{0,1:T(8,128)S(1)}, f32[64,8]{0,1:T(8,128)}, u32[]{:S(2)}) copy-start(f32[64,8]{0,1:T(8,128)} %param.34) | copy-start | bytes 6148
  4.3 21.7 %copy-start.27 = (s32[9]{0:T(128)S(1)}, s32[9]{0:T(128)}, u32[]{:S(2)}) copy-start(s32[9]{0:T(128)} %constant.757) | copy-start | bytes 112
  4.3 21.7 %copy-start.29 = (f32[9]{0:T(128)S(1)}, f32[9]{0:T(128)}, u32[]{:S(2)}) copy-start(f32[9]{0:T(128)} %constant.758) | copy-start | bytes 112
  4.4 11.4 %collective-permute-start = (f32[67,64]{1,0:T(8,128)S(1)}, f32[67,64]{1,0:T(8,128)S(1)}, u32[]{:S(2)}, u32[]{:S(2)}) collective-permute-start(f32[67,64]{1,0:T(8,128)S(1)} %get-tuple-element.842), channel_id=1, source_target_pairs={{0,16},{16,32},{32,48},{48,64},{64,80},{80,96},{96,112},{112,128},... | collective-permute-start | bytes 51464 | tf_op jit(solution)/shard_map/ppermute | solution.py:24
  7.8 8.3 %collective-permute-start.1 = (f32[67,64]{1,0:T(8,128)S(1)}, f32[67,64]{1,0:T(8,128)S(1)}, u32[]{:S(2)}, u32[]{:S(2)}) collective-permute-start(f32[67,64]{1,0:T(8,128)S(1)} %get-tuple-element.841), channel_id=1, source_target_pairs={{16,0},{32,16},{48,32},{64,48},{80,64},{96,80},{112,96},{128,112},... | collective-permute-start | bytes 51464 | tf_op jit(solution)/shard_map/ppermute | solution.py:27
  15.2 91.2 %copy-start.40 = (s32[64]{0:T(128)}, s32[64]{0:T(128)S(1)}, u32[]{:S(2)}) copy-start(s32[64]{0:T(128)S(1)} %compare_select_fusion) | copy-start | bytes 772
  15.8 10.2 %copy-start.37 = (pred[64]{0:T(512)(128)(4,1)}, pred[64]{0:T(512)(128)(4,1)S(1)}, u32[]{:S(2)}) copy-start(pred[64]{0:T(512)(128)(4,1)S(1)} %compare_and_fusion) | copy-start | bytes 196
  15.8 10.2 %copy-start.35 = (s32[1024]{0:T(1024)}, s32[1024]{0:T(1024)S(1)}, u32[]{:S(2)}) copy-start(s32[1024]{0:T(1024)S(1)} %pad_clamp_fusion.2) | copy-start | bytes 12292
  17.8 6.5 %collective-permute-start.2 = (f32[67,32]{1,0:T(8,128)S(1)}, f32[67,32]{1,0:T(8,128)S(1)}, u32[]{:S(2)}, u32[]{:S(2)}) collective-permute-start(f32[67,32]{1,0:T(8,128)S(1)} %get-tuple-element.840), channel_id=1, source_target_pairs={{0,1},{1,2},{2,3},{3,4},{4,5},{5,6},{6,7},{7,8},{8,9},{9,10},{10,1... | collective-permute-start | bytes 25736 | tf_op jit(solution)/shard_map/ppermute | solution.py:24
  19.7 6.2 %collective-permute-start.3 = (f32[67,32]{1,0:T(8,128)S(1)}, f32[67,32]{1,0:T(8,128)S(1)}, u32[]{:S(2)}, u32[]{:S(2)}) collective-permute-start(f32[67,32]{1,0:T(8,128)S(1)} %get-tuple-element.839), channel_id=1, source_target_pairs={{1,0},{2,1},{3,2},{4,3},{5,4},{6,5},{7,6},{8,7},{9,8},{10,9},{11,1... | collective-permute-start | bytes 25736 | tf_op jit(solution)/shard_map/ppermute | solution.py:27
  95.2 6.8 %collective-permute-start.5 = (f32[576,32]{0,1:T(8,128)S(1)}, f32[576,32]{0,1:T(8,128)S(1)}, u32[]{:S(2)}, u32[]{:S(2)}) collective-permute-start(f32[576,32]{0,1:T(8,128)S(1)} %get-tuple-element.827), channel_id=1, source_target_pairs={{1,0},{2,1},{3,2},{4,3},{5,4},{6,5},{7,6},{8,7},{9,8},{10,9},{11,1... | collective-permute-start | bytes 221192 | tf_op jit(solution)/shard_map/ppermute | solution.py:27
  99.7 6.7 %collective-permute-start.4 = (f32[576,32]{0,1:T(8,128)S(1)}, f32[576,32]{0,1:T(8,128)S(1)}, u32[]{:S(2)}, u32[]{:S(2)}) collective-permute-start(f32[576,32]{0,1:T(8,128)S(1)} %get-tuple-element.826), channel_id=1, source_target_pairs={{0,1},{1,2},{2,3},{3,4},{4,5},{5,6},{6,7},{7,8},{8,9},{9,10},{10,1... | collective-permute-start | bytes 221192 | tf_op jit(solution)/shard_map/ppermute | solution.py:24
  107.7 11.7 %collective-permute-start.7 = (f32[576,64]{0,1:T(8,128)S(1)}, f32[576,64]{0,1:T(8,128)S(1)}, u32[]{:S(2)}, u32[]{:S(2)}) collective-permute-start(f32[576,64]{0,1:T(8,128)S(1)} %get-tuple-element.829), channel_id=1, source_target_pairs={{16,0},{32,16},{48,32},{64,48},{80,64},{96,80},{112,96},{128,112},... | collective-permute-start | bytes 442376 | tf_op jit(solution)/shard_map/ppermute | solution.py:27
  116.2 11.5 %collective-permute-start.6 = (f32[576,64]{0,1:T(8,128)S(1)}, f32[576,64]{0,1:T(8,128)S(1)}, u32[]{:S(2)}, u32[]{:S(2)}) collective-permute-start(f32[576,64]{0,1:T(8,128)S(1)} %get-tuple-element.828), channel_id=1, source_target_pairs={{0,16},{16,32},{32,48},{48,64},{64,80},{80,96},{96,112},{112,128},... | collective-permute-start | bytes 442376 | tf_op jit(solution)/shard_map/ppermute | solution.py:24
  132.6 11.5 %collective-permute-start.8 = (f32[576,64]{0,1:T(8,128)S(1)}, f32[576,64]{0,1:T(8,128)S(1)}, u32[]{:S(2)}, u32[]{:S(2)}) collective-permute-start(f32[576,64]{0,1:T(8,128)S(1)} %get-tuple-element.831), channel_id=1, source_target_pairs={{0,16},{16,32},{32,48},{48,64},{64,80},{80,96},{96,112},{112,128},... | collective-permute-start | bytes 442376 | tf_op jit(solution)/shard_map/ppermute | solution.py:24
  134.5 14.5 %collective-permute-start.9 = (f32[576,64]{0,1:T(8,128)S(1)}, f32[576,64]{0,1:T(8,128)S(1)}, u32[]{:S(2)}, u32[]{:S(2)}) collective-permute-start(f32[576,64]{0,1:T(8,128)S(1)} %get-tuple-element.830), channel_id=1, source_target_pairs={{16,0},{32,16},{48,32},{64,48},{80,64},{96,80},{112,96},{128,112},... | collective-permute-start | bytes 442376 | tf_op jit(solution)/shard_map/ppermute | solution.py:27
  150.0 7.0 %collective-permute-start.10 = (f32[576,32]{0,1:T(8,128)S(1)}, f32[576,32]{0,1:T(8,128)S(1)}, u32[]{:S(2)}, u32[]{:S(2)}) collective-permute-start(f32[576,32]{0,1:T(8,128)S(1)} %get-tuple-element.833), channel_id=1, source_target_pairs={{0,1},{1,2},{2,3},{3,4},{4,5},{5,6},{6,7},{7,8},{8,9},{9,10},{10,1... | collective-permute-start | bytes 221192 | tf_op jit(solution)/shard_map/ppermute | solution.py:24
  151.9 6.6 %collective-permute-start.11 = (f32[576,32]{0,1:T(8,128)S(1)}, f32[576,32]{0,1:T(8,128)S(1)}, u32[]{:S(2)}, u32[]{:S(2)}) collective-permute-start(f32[576,32]{0,1:T(8,128)S(1)} %get-tuple-element.832), channel_id=1, source_target_pairs={{1,0},{2,1},{3,2},{4,3},{5,4},{6,5},{7,6},{8,7},{9,8},{10,9},{11,1... | collective-permute-start | bytes 221192 | tf_op jit(solution)/shard_map/ppermute | solution.py:27
  160.5 4.7 %copy-start.23 = (f32[64,8]{0,1:T(8,128)}, f32[64,8]{0,1:T(8,128)S(1)}, u32[]{:S(2)}) copy-start(f32[64,8]{0,1:T(8,128)S(1)} %get-tuple-element.1143) | copy-start | bytes 6148 | tf_op jit(solution)/shard_map/while
  160.5 8.0 %copy-start.5 = (f32[192,64]{0,1:T(8,128)}, f32[192,64]{0,1:T(8,128)S(1)}, u32[]{:S(2)}) copy-start(f32[192,64]{0,1:T(8,128)S(1)} %get-tuple-element.1144) | copy-start | bytes 147460 | tf_op jit(solution)/shard_map/while
  161.3 3.9 %copy-start.15 = (s32[1,512]{1,0:T(1,128)}, s32[1,512]{1,0:T(1,128)S(1)}, u32[]{:S(2)}) copy-start(s32[1,512]{1,0:T(1,128)S(1)} %get-tuple-element.1016) | copy-start | bytes 6148 | tf_op jit(solution)/shard_map/while
  165.2 3.3 copy-start.17
  171.5 3.2 copy-start.3
  180.7 3.3 copy-start.14
  185.4 4.7 %copy-start.23 = (f32[64,8]{0,1:T(8,128)}, f32[64,8]{0,1:T(8,128)S(1)}, u32[]{:S(2)}) copy-start(f32[64,8]{0,1:T(8,128)S(1)} %get-tuple-element.1143) | copy-start | bytes 6148 | tf_op jit(solution)/shard_map/while
  185.4 8.0 %copy-start.5 = (f32[192,64]{0,1:T(8,128)}, f32[192,64]{0,1:T(8,128)S(1)}, u32[]{:S(2)}) copy-start(f32[192,64]{0,1:T(8,128)S(1)} %get-tuple-element.1144) | copy-start | bytes 147460 | tf_op jit(solution)/shard_map/while
  186.2 3.9 %copy-start.15 = (s32[1,512]{1,0:T(1,128)}, s32[1,512]{1,0:T(1,128)S(1)}, u32[]{:S(2)}) copy-start(s32[1,512]{1,0:T(1,128)S(1)} %get-tuple-element.1016) | copy-start | bytes 6148 | tf_op jit(solution)/shard_map/while
  190.1 3.3 copy-start.17
  196.4 3.2 copy-start.3
  205.6 3.3 copy-start.14
  210.3 4.7 %copy-start.23 = (f32[64,8]{0,1:T(8,128)}, f32[64,8]{0,1:T(8,128)S(1)}, u32[]{:S(2)}) copy-start(f32[64,8]{0,1:T(8,128)S(1)} %get-tuple-element.1143) | copy-start | bytes 6148 | tf_op jit(solution)/shard_map/while
  210.3 8.0 %copy-start.5 = (f32[192,64]{0,1:T(8,128)}, f32[192,64]{0,1:T(8,128)S(1)}, u32[]{:S(2)}) copy-start(f32[192,64]{0,1:T(8,128)S(1)} %get-tuple-element.1144) | copy-start | bytes 147460 | tf_op jit(solution)/shard_map/while
  211.1 3.9 %copy-start.15 = (s32[1,512]{1,0:T(1,128)}, s32[1,512]{1,0:T(1,128)S(1)}, u32[]{:S(2)}) copy-start(s32[1,512]{1,0:T(1,128)S(1)} %get-tuple-element.1016) | copy-start | bytes 6148 | tf_op jit(solution)/shard_map/while
  215.0 3.3 copy-start.17
  230.5 3.3 copy-start.14
  235.2 4.7 %copy-start.23 = (f32[64,8]{0,1:T(8,128)}, f32[64,8]{0,1:T(8,128)S(1)}, u32[]{:S(2)}) copy-start(f32[64,8]{0,1:T(8,128)S(1)} %get-tuple-element.1143) | copy-start | bytes 6148 | tf_op jit(solution)/shard_map/while
  235.2 8.0 %copy-start.5 = (f32[192,64]{0,1:T(8,128)}, f32[192,64]{0,1:T(8,128)S(1)}, u32[]{:S(2)}) copy-start(f32[192,64]{0,1:T(8,128)S(1)} %get-tuple-element.1144) | copy-start | bytes 147460 | tf_op jit(solution)/shard_map/while
  236.1 3.9 %copy-start.15 = (s32[1,512]{1,0:T(1,128)}, s32[1,512]{1,0:T(1,128)S(1)}, u32[]{:S(2)}) copy-start(s32[1,512]{1,0:T(1,128)S(1)} %get-tuple-element.1016) | copy-start | bytes 6148 | tf_op jit(solution)/shard_map/while
  239.9 3.3 copy-start.17
  246.2 3.2 copy-start.3
  255.4 3.3 copy-start.14
  260.1 4.7 %copy-start.23 = (f32[64,8]{0,1:T(8,128)}, f32[64,8]{0,1:T(8,128)S(1)}, u32[]{:S(2)}) copy-start(f32[64,8]{0,1:T(8,128)S(1)} %get-tuple-element.1143) | copy-start | bytes 6148 | tf_op jit(solution)/shard_map/while
  260.1 8.0 %copy-start.5 = (f32[192,64]{0,1:T(8,128)}, f32[192,64]{0,1:T(8,128)S(1)}, u32[]{:S(2)}) copy-start(f32[192,64]{0,1:T(8,128)S(1)} %get-tuple-element.1144) | copy-start | bytes 147460 | tf_op jit(solution)/shard_map/while
  261.0 3.9 %copy-start.15 = (s32[1,512]{1,0:T(1,128)}, s32[1,512]{1,0:T(1,128)S(1)}, u32[]{:S(2)}) copy-start(s32[1,512]{1,0:T(1,128)S(1)} %get-tuple-element.1016) | copy-start | bytes 6148 | tf_op jit(solution)/shard_map/while
  264.8 3.3 copy-start.17
  271.2 3.2 copy-start.3
  280.3 3.3 copy-start.14
  285.0 4.7 %copy-start.23 = (f32[64,8]{0,1:T(8,128)}, f32[64,8]{0,1:T(8,128)S(1)}, u32[]{:S(2)}) copy-start(f32[64,8]{0,1:T(8,128)S(1)} %get-tuple-element.1143) | copy-start | bytes 6148 | tf_op jit(solution)/shard_map/while
  285.0 8.0 %copy-start.5 = (f32[192,64]{0,1:T(8,128)}, f32[192,64]{0,1:T(8,128)S(1)}, u32[]{:S(2)}) copy-start(f32[192,64]{0,1:T(8,128)S(1)} %get-tuple-element.1144) | copy-start | bytes 147460 | tf_op jit(solution)/shard_map/while
  285.9 3.9 %copy-start.15 = (s32[1,512]{1,0:T(1,128)}, s32[1,512]{1,0:T(1,128)S(1)}, u32[]{:S(2)}) copy-start(s32[1,512]{1,0:T(1,128)S(1)} %get-tuple-element.1016) | copy-start | bytes 6148 | tf_op jit(solution)/shard_map/while
  289.7 3.3 copy-start.17
  305.2 3.3 copy-start.14
  309.9 4.7 %copy-start.23 = (f32[64,8]{0,1:T(8,128)}, f32[64,8]{0,1:T(8,128)S(1)}, u32[]{:S(2)}) copy-start(f32[64,8]{0,1:T(8,128)S(1)} %get-tuple-element.1143) | copy-start | bytes 6148 | tf_op jit(solution)/shard_map/while
  309.9 8.0 %copy-start.5 = (f32[192,64]{0,1:T(8,128)}, f32[192,64]{0,1:T(8,128)S(1)}, u32[]{:S(2)}) copy-start(f32[192,64]{0,1:T(8,128)S(1)} %get-tuple-element.1144) | copy-start | bytes 147460 | tf_op jit(solution)/shard_map/while
  310.8 3.9 %copy-start.15 = (s32[1,512]{1,0:T(1,128)}, s32[1,512]{1,0:T(1,128)S(1)}, u32[]{:S(2)}) copy-start(s32[1,512]{1,0:T(1,128)S(1)} %get-tuple-element.1016) | copy-start | bytes 6148 | tf_op jit(solution)/shard_map/while
  314.6 3.3 copy-start.17
  330.1 3.3 copy-start.14
  335.7 8.2 %collective-permute-start.13 = (f32[3,32]{1,0:T(4,128)S(1)}, f32[3,32]{1,0:T(4,128)S(1)}, u32[]{:S(2)}, u32[]{:S(2)}) collective-permute-start(f32[3,32]{1,0:T(4,128)S(1)} %get-tuple-element.844), channel_id=1, source_target_pairs={{1,0},{2,1},{3,2},{4,3},{5,4},{6,5},{7,6},{8,7},{9,8},{10,9},{11,1... | collective-permute-start | bytes 1160 | tf_op jit(solution)/shard_map/ppermute | solution.py:27
  340.3 5.8 %collective-permute-start.12 = (f32[3,32]{1,0:T(4,128)S(1)}, f32[3,32]{1,0:T(4,128)S(1)}, u32[]{:S(2)}, u32[]{:S(2)}) collective-permute-start(f32[3,32]{1,0:T(4,128)S(1)} %get-tuple-element.843), channel_id=1, source_target_pairs={{0,1},{1,2},{2,3},{3,4},{4,5},{5,6},{6,7},{7,8},{8,9},{9,10},{10,1... | collective-permute-start | bytes 1160 | tf_op jit(solution)/shard_map/ppermute | solution.py:24
  347.4 12.1 %collective-permute-start.15 = (f32[3,64]{0,1:T(8,128)S(1)}, f32[3,64]{0,1:T(8,128)S(1)}, u32[]{:S(2)}, u32[]{:S(2)}) collective-permute-start(f32[3,64]{0,1:T(8,128)S(1)} %get-tuple-element.835), channel_id=1, source_target_pairs={{16,0},{32,16},{48,32},{64,48},{80,64},{96,80},{112,96},{128,112},... | collective-permute-start | bytes 2312 | tf_op jit(solution)/shard_map/ppermute | solution.py:27
  356.1 10.0 %collective-permute-start.14 = (f32[3,64]{0,1:T(8,128)S(1)}, f32[3,64]{0,1:T(8,128)S(1)}, u32[]{:S(2)}, u32[]{:S(2)}) collective-permute-start(f32[3,64]{0,1:T(8,128)S(1)} %get-tuple-element.834), channel_id=1, source_target_pairs={{0,16},{16,32},{32,48},{48,64},{64,80},{80,96},{96,112},{112,128},... | collective-permute-start | bytes 2312 | tf_op jit(solution)/shard_map/ppermute | solution.py:24
  (158 other events, 274.5 us)
where the time goes:
time: 372 us; the launch traced here: 368 us
  other arithmetic  121 us (33%)
  matrix products  83.9 us (23%)
  starting transfers between devices  67.2 us (18%)
  local copies, waits for them, and re-layouts  58 us (16%)
  waiting for transfers between devices  32.7 us (9%)
  loops' own time  4.11 us (1%)
    ppermute x8, starting transfers between devices, padded(): lax.ppermute(lax.slice_in_dim(block, 0, width, axis=dim), axis, backward)  50.4 us
    dot_general x42, matrix products, pick_rows(): lax.dot_general(rows_data, table, (((1,), (0,)), ((), ())), precision=hig...  36.5 us
    dot_general x28, matrix products, place_rows(): lax.dot_general(values, table, (((1,), (1,)), ((), ())), precision=highes...  27.6 us
    ppermute x8, waiting for transfers between devices, padded(): lax.ppermute(lax.slice_in_dim(block, block.shape[dim] - width, None, axis...  23 us
    scatter-add x7, other arithmetic, edge_messages(): radial = radial.reshape(3, channels, edge_total)[degree_of]  20 us
    reduce_sum x7, other arithmetic, edge_messages(): (shapes * parity_sign[:, None])[:, None, :] * radial * own_features[None]  19.7 us
    while x378, local copies, waits for them, and re-layouts  16.9 us
    ppermute x8, starting transfers between devices, padded(): lax.ppermute(lax.slice_in_dim(block, block.shape[dim] - width, None, axis...  16.8 us
  transfers between devices with their start and end apart: 16, of which 11 were waited for; matrix products, arithmetic and copies ran while one was open for 1% of the time, Pallas kernels for 0%

commit v1 on v0

v1 whole, which is shorter than its diff:
```python
import functools
import math

import jax
import jax.numpy as jnp
from jax import lax
from jax.experimental import pallas as pl
from jax.experimental.pallas import tpu as pltpu
from jax.sharding import PartitionSpec as P

MESH = pl.DeviceIdType.MESH
F32 = jnp.float32
BF16 = jnp.bfloat16
HIGHEST = lax.Precision.HIGHEST

CH = 64
OWN = 128
GX = 64
GY = 32
EXT = 320
EXT_PAD = 384
TILE = 256
STEPS = 13
SLOTS = TILE * STEPS
ROWS = 9 * CH
ROWS_PAD = 640

CUTOFF = 5.0
SCALE = 0.3
S3 = math.sqrt(3.0)
S5 = math.sqrt(5.0)
S15 = math.sqrt(15.0)
DEGREE = (0, 1, 1, 1, 2, 2, 2, 2, 2)
PARITY = (1.0, -1.0, -1.0, -1.0, 1.0, 1.0, 1.0, 1.0, 1.0)

NN = (((1,), (0,)), ((), ()))
NT = (((1,), (1,)), ((), ()))


def mm(a, b, dims=NN, precision=None):
    return lax.dot_general(a, b, dims, precision=precision, preferred_element_type=F32)


def split2(x):
    hi = x.astype(BF16)
    return hi, (x - hi.astype(F32)).astype(BF16)


def split3(x):
    a = x.astype(BF16).astype(F32)
    b = (x - a).astype(BF16).astype(F32)
    return a, b, (x - a) - b


def iota(shape, dim):
    return lax.broadcasted_iota(jnp.int32, shape, dim)


def onehot(cond):
    return jnp.where(cond, 1.0, 0.0)


def sin_cos(arg):
    k = jnp.floor(arg * (1.0 / math.pi) + 0.5)
    r = (arg - k * 3.140625) - k * (math.pi - 3.140625)
    sign = 1.0 - 2.0 * (k - 2.0 * jnp.floor(k * 0.5))
    r2 = r * r
    s = 1.0 / 6227020800.0
    for c in (-1.0 / 39916800, 1.0 / 362880, -1.0 / 5040, 1.0 / 120, -1.0 / 6, 1.0):
        s = s * r2 + c
    q = -1.0 / 87178291200.0
    for c in (1.0 / 479001600, -1.0 / 3628800, 1.0 / 40320, -1.0 / 720, 1.0 / 24, -0.5, 1.0):
        q = q * r2 + c
    return sign * (s * r), sign * q


def body(
    comm,
    n_gx,
    n_gy,
    pos_ref,
    feat_ref,
    spec_ref,
    edge_ref,
    cnt_ref,
    slx_ref,
    sly_ref,
    win_ref,
    wout_ref,
    mix_ref,
    outw_ref,
    se_ref,
    energy_ref,
    force_ref,
    pos8,
    slyp,
    oh1,
    oh2,
    send_a,
    recv_a,
    ext_l,
    pa_s,
    fa_s,
    fb_s,
    geo,
    r_s,
    rp_s,
    w3,
    m_s,
    s1,
    s2,
    rsy,
    rsx,
    gown,
    gext,
    sgx,
    rgx,
    sgy,
    rgy,
    zacc,
    facc,
    send_f,
    recv_f,
    send_sem,
    recv_sem,
):
    if comm:
        ix = lax.axis_index("gx")
        iy = lax.axis_index("gy")
        x_low = (lax.rem(ix + n_gx - 1, n_gx), iy)
        x_high = (lax.rem(ix + 1, n_gx), iy)
        y_low = (ix, lax.rem(iy + n_gy - 1, n_gy))
        y_high = (ix, lax.rem(iy + 1, n_gy))
        barrier = pltpu.get_barrier_semaphore()
        for device in (x_low, x_high, y_low, y_high):
            pl.semaphore_signal(barrier, inc=1, device_id=device, device_id_type=MESH)
    else:
        x_low = x_high = y_low = y_high = None

    def push(number, src, dst, device):
        if not comm:
            return None
        copy = pltpu.make_async_remote_copy(
            src_ref=src,
            dst_ref=dst,
            send_sem=send_sem.at[number],
            recv_sem=recv_sem.at[number],
            device_id=device,
            device_id_type=MESH,
        )
        copy.start()
        return copy

    def settle(*copies):
        for copy in copies:
            if copy is not None:
                copy.wait()

    lane = iota((1, OWN), 1)

    slyp[...] = jnp.full_like(slyp, -1)
    slyp[:, 0 : 2 * GY] = sly_ref[...]
    ohx_t32 = onehot(iota((OWN, OWN), 0) == slx_ref[...])
    ohy_t32 = onehot(iota((2 * OWN, OWN), 0) == slyp[...])
    ohx_t = ohx_t32.astype(BF16)
    ohy_t = ohy_t32.astype(BF16)
    ohx = ohx_t32.T.astype(BF16)
    ohy = ohy_t32.T.astype(BF16)

    def pack(rows72):
        a, b, c = split3(rows72[CH : CH + 8])
        pieces = jnp.concatenate([a, b, c, jnp.zeros_like(a)], axis=0).astype(BF16)
        return jnp.concatenate([rows72[:CH].astype(BF16), pieces], axis=0)

    def unpack(rows96):
        return (rows96[CH : CH + 8] + rows96[CH + 8 : CH + 16]) + rows96[CH + 16 : CH + 24]

    def fold_x(low, high):
        return jnp.where(lane < GX, pltpu.roll(low, GX, 1), pltpu.roll(high, GX, 1))

    def fold_y(low, high):
        picked = jnp.where(lane < GY, pltpu.roll(low, OWN - GY, 1), pltpu.roll(high, GY, 1))
        return jnp.where(lane < 2 * GY, picked, 0.0)

    pos8[...] = jnp.zeros_like(pos8)
    pos8[0:3, :] = pos_ref[...]
    own_l = pack(jnp.concatenate([feat_ref[...].astype(F32), pos8[...]], axis=0))
    ext_l[:, 0:OWN] = own_l
    picked = mm(own_l, ohx_t)
    send_a[0, 0:CH, :] = picked[0:CH]
    send_a[0, CH : CH + 8, :] = unpack(picked)
    if comm:
        pl.semaphore_wait(barrier, 4)
    c0 = push(0, send_a.at[0], recv_a.at[1], x_low)
    c1 = push(1, send_a.at[0], recv_a.at[0], x_high)

    w_hi, w_lo = split2(wout_ref[...])
    col = iota((CH, 3 * CH), 1)
    row = iota((CH, 3 * CH), 0)
    place_hi = onehot((col == row) | (col == row + CH)).astype(BF16)
    place_lo = onehot(col == row + 2 * CH).astype(BF16)
    w3[...] = (mm(w_hi, place_hi) + mm(w_lo, place_lo)).astype(BF16)
    count = cnt_ref[0]

    def table_step(step, carry):
        at = pl.ds(pl.multiple_of(step * TILE, TILE), TILE)
        live = iota((1, TILE), 1) + step * TILE < count
        first = jnp.where(live, edge_ref[0:1, at], -1)
        second = jnp.where(live, edge_ref[1:2, at], -1)
        table1 = onehot(iota((OWN, TILE), 0) == first).astype(BF16)
        oh1[:, at] = table1
        oh2[:, at] = onehot(iota((EXT_PAD, TILE), 0) == second).astype(BF16)
        got = mm(ext_l[:, 0:OWN], table1)
        fa_s[:, at] = got[0:CH]
        pa_s[:, at] = unpack(got)
        return carry

    lax.fori_loop(0, STEPS, table_step, 0)

    settle(c0, c1)
    if comm:
        section = pack(fold_x(recv_a[0], recv_a[1]))
    else:
        section = own_l
    ext_l[:, OWN : 2 * OWN] = section
    picked = mm(own_l, ohy_t[0:OWN]) + mm(section, ohy_t[OWN : 2 * OWN])
    send_a[1, 0:CH, :] = picked[0:CH]
    send_a[1, CH : CH + 8, :] = unpack(picked)
    c0 = push(2, send_a.at[1], recv_a.at[3], y_low)
    c1 = push(3, send_a.at[1], recv_a.at[2], y_high)
    settle(c0, c1)
    if comm:
        ext_l[:, 2 * OWN : 3 * OWN] = pack(fold_y(recv_a[2], recv_a[3]))
    else:
        ext_l[:, 2 * OWN : 3 * OWN] = jnp.where(lane < 2 * GY, own_l, 0.0)

    s1[...] = jnp.zeros_like(s1)
    s2[...] = jnp.zeros_like(s2)
    m_s[ROWS:ROWS_PAD, :] = jnp.zeros((ROWS_PAD - ROWS, TILE), BF16)
    m_s[ROWS_PAD + ROWS :, :] = jnp.zeros((ROWS_PAD - ROWS, TILE), BF16)

    def messages(shapes, radial, features):
        for degree in range(3):
            product = radial[degree * CH : (degree + 1) * CH] * features
            for q in range(9):
                if DEGREE[q] != degree:
                    continue
                hi, lo = split2(shapes[q] * product)
                m_s[q * CH : (q + 1) * CH, :] = hi
                m_s[ROWS_PAD + q * CH : ROWS_PAD + (q + 1) * CH, :] = lo

    def first_step(step, carry):
        at = pl.ds(pl.multiple_of(step * TILE, TILE), TILE)
        live = iota((1, TILE), 1) + step * TILE < count
        got = mm(ext_l[...], oh2[:, at])
        fb_s[:, at] = got[0:CH]
        relative = unpack(got) - pa_s[:, at]
        rx = jnp.where(live, relative[0:1], 2.0)
        ry = jnp.where(live, relative[1:2], 0.0)
        rz = jnp.where(live, relative[2:3], 0.0)
        d = jnp.sqrt(rx * rx + ry * ry + rz * rz)
        inv = 1.0 / d
        x, y, z = rx * inv, ry * inv, rz * inv
        scaled = d * (1.0 / CUTOFF)
        left = 1.0 - scaled * scaled
        inside = d < CUTOFF
        env = jnp.where(inside, left * left, 0.0)
        env_d = jnp.where(inside, (-4.0 / CUTOFF) * scaled * left, 0.0)
        shapes = [
            jnp.full_like(x, SCALE),
            (SCALE * S3) * x,
            (SCALE * S3) * y,
            (SCALE * S3) * z,
            (SCALE * S15) * (x * y),
            (SCALE * S15) * (y * z),
            (SCALE * 0.5 * S5) * (3.0 * z * z - 1.0),
            (SCALE * S15) * (x * z),
            (SCALE * 0.5 * S15) * (x * x - y * y),
        ]
        for number, value in enumerate(shapes + [x, y, z, inv]):
            geo[number : number + 1, at] = value
        order = (iota((8, TILE), 0) + 1).astype(F32)
        sine, cosine = sin_cos(order * (d * (math.pi / CUTOFF)))
        root = math.sqrt(2.0 / CUTOFF)
        bessel = root * sine * inv
        bessel_d = (root * (math.pi / CUTOFF) * order * cosine - bessel) * inv
        both = mm(win_ref[...], jnp.concatenate([bessel, bessel_d], axis=1), precision=HIGHEST)
        u, u_d = both[:, :TILE], both[:, TILE:]
        gate = 1.0 / (1.0 + jnp.exp(-u))
        hidden = u * gate
        slope = gate * (1.0 + u * (1.0 - gate))
        g = jnp.concatenate([env * hidden, env_d * hidden + env * (slope * u_d)], axis=1)
        hi, lo = split2(g)
        radial = mm(w3[...], jnp.concatenate([hi, lo, hi], axis=0))
        r_s[:, at] = radial[:, :TILE]
        rp_s[:, at] = radial[:, TILE:]
        messages(
            [PARITY[q] * shapes[q] for q in range(9)], radial[:, :TILE], fa_s[:, at]
        )
        out = mm(oh2[0:EXT, at], m_s[...], NT)
        s2[...] += out[:, :ROWS] + out[:, ROWS_PAD : ROWS_PAD + ROWS]
        return carry

    lax.fori_loop(0, STEPS, first_step, 0)

    c0 = push(4, s2.at[pl.ds(2 * OWN, GY)], rsy.at[pl.ds(GY, GY)], y_low)
    c1 = push(5, s2.at[pl.ds(2 * OWN + GY, GY)], rsy.at[pl.ds(0, GY)], y_high)

    def second_step(step, carry):
        at = pl.ds(pl.multiple_of(step * TILE, TILE), TILE)
        messages([geo[q : q + 1, at] for q in range(9)], r_s[:, at], fb_s[:, at])
        out = mm(oh1[:, at], m_s[...], NT)
        s1[...] += out[:, :ROWS] + out[:, ROWS_PAD : ROWS_PAD + ROWS]
        return carry

    lax.fori_loop(0, STEPS // 2, second_step, 0)
    settle(c0, c1)
    if comm:
        hi, lo = split2(rsy[...])
        s2[0 : 2 * OWN, :] += mm(ohy_t[:, 0 : 2 * GY], hi) + mm(ohy_t[:, 0 : 2 * GY], lo)
    c0 = push(6, s2.at[pl.ds(OWN, GX)], rsx.at[pl.ds(GX, GX)], x_low)
    c1 = push(7, s2.at[pl.ds(OWN + GX, GX)], rsx.at[pl.ds(0, GX)], x_high)
    lax.fori_loop(STEPS // 2, STEPS, second_step, 0)
    settle(c0, c1)
    sums_t = s2[0:OWN, :] + s1[...]
    if comm:
        hi, lo = split2(rsx[...])
        sums_t = sums_t + mm(ohx_t, hi) + mm(ohx_t, lo)

    sums = sums_t.T
    squares = [sums[q * CH : (q + 1) * CH] * sums[q * CH : (q + 1) * CH] for q in range(9)]
    invariant = jnp.concatenate(
        [
            squares[0],
            squares[1] + squares[2] + squares[3],
            squares[4] + squares[5] + squares[6] + squares[7] + squares[8],
        ],
        axis=0,
    )
    mixed = mm(mix_ref[...], invariant, precision=HIGHEST) + feat_ref[...].astype(F32)
    gate = 1.0 / (1.0 + jnp.exp(-mixed))
    diagonal = iota((CH, CH), 0) == iota((CH, CH), 1)
    weight = jnp.sum(jnp.where(diagonal, outw_ref[...], 0.0), axis=1, keepdims=True)
    energy = jnp.sum(weight * (mixed * gate), axis=0, keepdims=True)
    kind = spec_ref[...]
    shift = jnp.zeros_like(energy)
    for k in range(5):
        shift = jnp.where(kind == k, se_ref[k], shift)
    energy_ref[...] = energy + shift
    d_mixed = weight * (gate * (1.0 + mixed * (1.0 - gate)))
    d_inv = 2.0 * mm(mix_ref[...].T, d_mixed, precision=HIGHEST)
    gext[...] = jnp.zeros_like(gext)
    for q in range(9):
        at = slice(q * CH, (q + 1) * CH)
        gradient = sums[at] * d_inv[DEGREE[q] * CH : (DEGREE[q] + 1) * CH]
        hi, lo = split2(gradient)
        gown[at, 0:OWN] = hi
        gown[at, OWN : 2 * OWN] = lo
        hi, lo = split2(PARITY[q] * gradient)
        gext[at, 0:OWN] = hi
        gext[at, EXT_PAD : EXT_PAD + OWN] = lo

    def own_rows(table):
        return mm(table, gext[:, 0:OWN], NT) + mm(table, gext[:, EXT_PAD : EXT_PAD + OWN], NT)

    sgx[...] = own_rows(ohx)
    c0 = push(8, sgx.at[pl.ds(0, GX)], rgx.at[pl.ds(GX, GX)], x_low)
    c1 = push(9, sgx.at[pl.ds(GX, GX)], rgx.at[pl.ds(0, GX)], x_high)
    outgoing_y = own_rows(ohy[0 : 2 * GY, 0:OWN])

    def store_ghosts(rows, start):
        hi, lo = split2(rows.T)
        count_here = rows.shape[0]
        gext[:, start : start + count_here] = hi
        gext[:, EXT_PAD + start : EXT_PAD + start + count_here] = lo

    def contract(step, gathered, features):
        at = pl.ds(pl.multiple_of(step * TILE, TILE), TILE)
        along = jnp.zeros((CH, TILE), F32)
        rows_z = []
        for degree in range(3):
            radial = r_s[degree * CH : (degree + 1) * CH, at]
            total = None
            for q in range(9):
                if DEGREE[q] != degree:
                    continue
                product = gathered[q * CH : (q + 1) * CH] * features
                rows_z.append(jnp.sum(radial * product, axis=0, keepdims=True))
                term = geo[q : q + 1, at] * product
                total = term if total is None else total + term
            along = along + rp_s[degree * CH : (degree + 1) * CH, at] * total
        rows_z.append(jnp.sum(along, axis=0, keepdims=True))
        return rows_z

    def own_step(step, carry):
        at = pl.ds(pl.multiple_of(step * TILE, TILE), TILE)
        table = oh1[:, at]
        gathered = mm(gown[...], jnp.concatenate([table, table], axis=0))
        rows_z = contract(step, gathered, fb_s[:, at])
        for number, value in enumerate(rows_z):
            zacc[number : number + 1, at] = value
        return carry

    lax.fori_loop(0, 8, own_step, 0)
    settle(c0, c1)
    if comm:
        hi, lo = split2(rgx[...])
        table = ohy[0 : 2 * GY, OWN : 2 * OWN]
        sgy[...] = outgoing_y + mm(table, hi) + mm(table, lo)
    c0 = push(10, sgy.at[pl.ds(0, GY)], rgy.at[pl.ds(GY, GY)], y_low)
    c1 = push(11, sgy.at[pl.ds(GY, GY)], rgy.at[pl.ds(0, GY)], y_high)
    if comm:
        store_ghosts(rgx[...], OWN)
    lax.fori_loop(8, STEPS, own_step, 0)
    settle(c0, c1)
    if comm:
        store_ghosts(rgy[...], 2 * OWN)

    facc[...] = jnp.zeros_like(facc)

    def last_step(step, carry):
        at = pl.ds(pl.multiple_of(step * TILE, TILE), TILE)
        table = oh2[:, at]
        gathered = mm(gext[...], jnp.concatenate([table, table], axis=0))
        rows_z = contract(step, gathered, fa_s[:, at])
        z = [rows_z[q] + zacc[q : q + 1, at] for q in range(10)]
        nx, ny, nz = geo[9:10, at], geo[10:11, at], geo[11:12, at]
        inv = geo[12:13, at]
        gx = S3 * z[1] + S15 * (ny * z[4] + nz * z[7] + nx * z[8])
        gy = S3 * z[2] + S15 * (nx * z[4] + nz * z[5] - ny * z[8])
        gz = S3 * z[3] + S15 * (ny * z[5] + nx * z[7]) + (3.0 * S5) * (nz * z[6])
        factor = SCALE * inv
        gx, gy, gz = gx * factor, gy * factor, gz * factor
        radial_part = z[9] - (gx * nx + gy * ny + gz * nz)
        zero = jnp.zeros((5, TILE), F32)
        pulled = jnp.concatenate(
            [gx + radial_part * nx, gy + radial_part * ny, gz + radial_part * nz, zero], axis=0
        )
        hi = pulled.astype(BF16).astype(F32)
        pieces = jnp.concatenate([hi, pulled - hi], axis=0).astype(BF16)
        facc[...] -= mm(table, pieces, NT)
        facc[0:OWN, :] += mm(oh1[:, at], pieces, NT)
        return carry

    lax.fori_loop(0, STEPS, last_step, 0)

    def home(rows8, table):
        a, b, c = split3(rows8)
        out = mm(jnp.concatenate([a, b, c, jnp.zeros_like(a)], axis=0).astype(BF16), table)
        return out[0:8] + out[8:16] + out[16:24]

    total = facc[...].T
    total = total[0:8] + total[8:16]
    send_f[0] = total[:, 2 * OWN : 3 * OWN]
    c0 = push(12, send_f.at[0], recv_f.at[1], y_low)
    c1 = push(13, send_f.at[0], recv_f.at[0], y_high)
    settle(c0, c1)
    near = total[:, 0 : 2 * OWN]
    if comm:
        near = near + home(fold_y(recv_f[0], recv_f[1]), ohy)
    send_f[1] = near[:, OWN : 2 * OWN]
    c0 = push(14, send_f.at[1], recv_f.at[3], x_low)
    c1 = push(15, send_f.at[1], recv_f.at[2], x_high)
    settle(c0, c1)
    own = near[:, 0:OWN]
    if comm:
        own = own + home(fold_x(recv_f[2], recv_f[3]), ohx)
    force_ref[...] = own[0:3]


def run(args, n_gx, n_gy, comm=True):
    (
        positions,
        features,
        species,
        edge_list,
        edge_count,
        send_list_x,
        send_list_y,
        radial_in,
        radial_out,
        mix_weight,
        out_weight,
        species_energy,
    ) = args
    vmem = pl.BlockSpec(memory_space=pltpu.VMEM)
    smem = pl.BlockSpec(memory_space=pltpu.SMEM)
    scratch = [
        pltpu.VMEM((8, OWN), F32),
        pltpu.VMEM((1, OWN), jnp.int32),
        pltpu.VMEM((OWN, SLOTS), BF16),
        pltpu.VMEM((EXT_PAD, SLOTS), BF16),
        pltpu.VMEM((2, CH + 8, OWN), F32),
        pltpu.VMEM((4, CH + 8, OWN), F32),
        pltpu.VMEM((CH + 32, EXT_PAD), BF16),
        pltpu.VMEM((8, SLOTS), F32),
        pltpu.VMEM((CH, SLOTS), F32),
        pltpu.VMEM((CH, SLOTS), F32),
        pltpu.VMEM((16, SLOTS), F32),
        pltpu.VMEM((3 * CH, SLOTS), F32),
        pltpu.VMEM((3 * CH, SLOTS), F32),
        pltpu.VMEM((3 * CH, 3 * CH), BF16),
        pltpu.VMEM((2 * ROWS_PAD, TILE), BF16),
        pltpu.VMEM((OWN, ROWS), F32),
        pltpu.VMEM((EXT, ROWS), F32),
        pltpu.VMEM((2 * GY, ROWS), F32),
        pltpu.VMEM((2 * GX, ROWS), F32),
        pltpu.VMEM((ROWS, 2 * OWN), BF16),
        pltpu.VMEM((ROWS, 2 * EXT_PAD), BF16),
        pltpu.VMEM((2 * GX, ROWS), F32),
        pltpu.VMEM((2 * GX, ROWS), F32),
        pltpu.VMEM((2 * GY, ROWS), F32),
        pltpu.VMEM((2 * GY, ROWS), F32),
        pltpu.VMEM((16, SLOTS), F32),
        pltpu.VMEM((EXT_PAD, 16), F32),
        pltpu.VMEM((2, 8, OWN), F32),
        pltpu.VMEM((4, 8, OWN), F32),
        pltpu.SemaphoreType.DMA((16,)),
        pltpu.SemaphoreType.DMA((16,)),
    ]
    params = {"collective_id": 0, "has_side_effects": True} if comm else {}
    energies, forces = pl.pallas_call(
        functools.partial(body, comm, n_gx, n_gy),
        out_shape=(
            jax.ShapeDtypeStruct((1, OWN), F32),
            jax.ShapeDtypeStruct((3, OWN), F32),
        ),
        in_specs=[vmem, vmem, vmem, vmem, smem, vmem, vmem, vmem, vmem, vmem, vmem, smem],
        out_specs=(vmem, vmem),
        scratch_shapes=scratch,
        compiler_params=pltpu.CompilerParams(vmem_limit_bytes=60 * 1024 * 1024, **params),
        name="layer",
    )(
        positions,
        features,
        species.reshape(1, -1),
        edge_list,
        edge_count,
        send_list_x.reshape(1, -1),
        send_list_y.reshape(1, -1),
        radial_in,
        radial_out,
        mix_weight,
        out_weight.reshape(1, -1),
        species_energy,
    )
    return energies.reshape(-1), forces


def solution(mesh):
    n_gx, n_gy = mesh.shape["gx"], mesh.shape["gy"]
    both = ("gx", "gy")
    placed = (
        P(None, both),
        P(None, both),
        P(both),
        P(None, both),
        P(both),
        P(both),
        P(both),
        P(),
        P(),
        P(),
        P(),
        P(),
    )
    return jax.shard_map(
        lambda *args: run(args, n_gx, n_gy),
        mesh=mesh,
        in_specs=placed,
        out_specs=(P(both), P(None, both)),
        check_vma=False,
    )
```

time: 372 us -> 86.8 us (0.23)
  the two profiles are of different devices: /device:TPU:136 before, /device:TPU:24 now
where the time goes in v1:
time: 86.8 us; the launch traced here: 86.6 us
  Pallas kernels  80.6 us (93%)
  local copies, waits for them, and re-layouts  4.63 us (5%)
  between operations  1.31 us (2%)
    pallas_call x1, Pallas kernels, run(): pl.pallas_call(functools.partial(body, comm, n_gx, n_gy), out_shape=(jax....  80.6 us
    unnamed x10, local copies, waits for them, and re-layouts  4.63 us

profile of v1, /device:TPU:24, one launch (start us, length us, event | category | flops | bytes accessed | tf_op | source)
XLA Modules:
  0.0 86.6 jit_solution(2940408317004747648)
XLA Ops:
  1.3 0.0 copy-start
  1.3 0.7 copy-done
  2.0 0.7 copy.14.win_ref
  2.7 1.6 %copy.15.wout_ref = f32[192,64]{1,0:T(8,128)} copy(f32[192,64]{0,1:T(8,128)} %param.20) | data formatting | bytes 98304 | tf_op args[8]
  4.2 80.6 %layer.1 = (f32[1,128]{1,0:T(1,128)}, f32[3,128]{1,0:T(4,128)}) custom-call(f32[3,128]{1,0:T(4,128)} %pos_ref.1, bf16[64,128]{1,0:T(8,128)(2,1)} %feat_ref.1, s32[1,128]{1,0:T(1,128)} %bitcast.5, s32[2,3584]{1,0:T(2,128)} %edge_ref.1, s32[1]{0:T(128)S(6)} %copy.18.cnt_ref, s32[1,128]{1,0:T(1,128)} %bitcast.6, s32[1,64]{1,0:T(1,128)} %bitcast.7, ...), custom_call_target="tpu_custom_call" | custom-call | tf_op jit(solution)/shard_map/layer/pallas_call | solution.py:522
  84.8 0.0 copy-start.2
  84.9 0.0 copy-start.1
  84.9 0.6 copy-done.2
  85.5 0.5 copy.19
  86.0 0.0 copy-done.1
  86.0 0.6 copy.20
Async XLA Ops:
  1.3 0.7 copy-start
  84.8 0.6 copy-start.2
  84.9 1.1 %copy-start.1 = (f32[3,128]{1,0:T(4,128)S(1)}, f32[3,128]{1,0:T(4,128)}, u32[]{:S(2)}) copy-start(f32[3,128]{1,0:T(4,128)} %get-tuple-element.9) | copy-start | bytes 4612

commit v2 on v1

--- a/solution.py
+++ b/solution.py
@@ -23,7 +23,7 @@
 STEPS = 13
 SLOTS = TILE * STEPS
 ROWS = 9 * CH
-ROWS_PAD = 640
+DENSE = 32
 
 CUTOFF = 5.0
 SCALE = 0.3
@@ -32,6 +32,11 @@
 S15 = math.sqrt(15.0)
 DEGREE = (0, 1, 1, 1, 2, 2, 2, 2, 2)
 PARITY = (1.0, -1.0, -1.0, -1.0, 1.0, 1.0, 1.0, 1.0, 1.0)
+
+UNROLL_GATHER = 1
+UNROLL_RADIAL = 1
+UNROLL_SUMS = 1
+UNROLL_BACK = 1
 
 NN = (((1,), (0,)), ((), ()))
 NT = (((1,), (1,)), ((), ()))
@@ -100,12 +105,17 @@
     recv_a,
     ext_l,
     pa_s,
+    rel_d,
+    bes_d,
+    slope_d,
+    geo_d,
+    pull_d,
     fa_s,
     fb_s,
-    geo,
     r_s,
     rp_s,
     w3,
+    w6,
     m_s,
     s1,
     s2,
@@ -117,8 +127,9 @@
     rgx,
     sgy,
     rgy,
-    zacc,
-    facc,
+    z_own,
+    z_ext,
+    pieces_s,
     send_f,
     recv_f,
     send_sem,
@@ -194,12 +205,12 @@
     c0 = push(0, send_a.at[0], recv_a.at[1], x_low)
     c1 = push(1, send_a.at[0], recv_a.at[0], x_high)
 
-    w_hi, w_lo = split2(wout_ref[...])
-    col = iota((CH, 3 * CH), 1)
-    row = iota((CH, 3 * CH), 0)
-    place_hi = onehot((col == row) | (col == row + CH)).astype(BF16)
-    place_lo = onehot(col == row + 2 * CH).astype(BF16)
-    w3[...] = (mm(w_hi, place_hi) + mm(w_lo, place_lo)).astype(BF16)
+    hi, lo = split2(wout_ref[...])
+    hi, lo = hi.astype(F32), lo.astype(F32)
+    w3[...] = jnp.concatenate([hi, hi, lo], axis=0).T.astype(BF16)
+    a, b, c = split3(win_ref[...])
+    zero = jnp.zeros_like(a)
+    w6[...] = jnp.concatenate([a, a, b, b, a, c, zero, zero], axis=0).T.astype(BF16)
     count = cnt_ref[0]
 
     def table_step(step, carry):
@@ -234,100 +245,156 @@
     else:
         ext_l[:, 2 * OWN : 3 * OWN] = jnp.where(lane < 2 * GY, own_l, 0.0)
 
-    s1[...] = jnp.zeros_like(s1)
-    s2[...] = jnp.zeros_like(s2)
-    m_s[ROWS:ROWS_PAD, :] = jnp.zeros((ROWS_PAD - ROWS, TILE), BF16)
-    m_s[ROWS_PAD + ROWS :, :] = jnp.zeros((ROWS_PAD - ROWS, TILE), BF16)
-
-    def messages(shapes, radial, features):
+    def span(step):
+        return pl.ds(pl.multiple_of(step * TILE, TILE), TILE)
+
+    def loop(start, stop, step_fn, unroll):
+        def one(step, carry):
+            step_fn(step)
+            return carry
+
+        lax.fori_loop(start, stop, one, 0, unroll=unroll)
+
+    def halves(value):
+        return value[:, 0:OWN], value[:, OWN:TILE]
+
+    def get_row(ref, number, step):
+        at = number * DENSE + 2 * step
+        return jnp.concatenate([ref[pl.ds(at, 1), :], ref[pl.ds(at + 1, 1), :]], axis=1)
+
+    def put_row(ref, number, step, value):
+        at = number * DENSE + 2 * step
+        low, high = halves(value)
+        ref[pl.ds(at, 1), :] = low
+        ref[pl.ds(at + 1, 1), :] = high
+
+    def get_eight(ref, step):
+        at = 2 * step
+        return jnp.concatenate(
+            [ref[pl.ds(at, 8, stride=DENSE), :], ref[pl.ds(at + 1, 8, stride=DENSE), :]], axis=1
+        )
+
+    def dense(ref, number):
+        return ref[number * DENSE : (number + 1) * DENSE, :]
+
+    rel_d[...] = jnp.full_like(rel_d, 2.0)
+
+    def gather_step(step):
+        got = mm(ext_l[...], oh2[:, span(step)])
+        fb_s[:, span(step)] = got[0:CH]
+        relative = unpack(got) - pa_s[:, span(step)]
+        for number in range(3):
+            put_row(rel_d, number, step, relative[number : number + 1])
+
+    loop(0, STEPS, gather_step, UNROLL_GATHER)
+
+    live = iota((DENSE, OWN), 0) * OWN + iota((DENSE, OWN), 1) < count
+    rx = jnp.where(live, dense(rel_d, 0), 2.0)
+    ry = jnp.where(live, dense(rel_d, 1), 0.0)
+    rz = jnp.where(live, dense(rel_d, 2), 0.0)
+    d = jnp.sqrt(rx * rx + ry * ry + rz * rz)
+    inv = 1.0 / d
+    x, y, z = rx * inv, ry * inv, rz * inv
+    scaled = d * (1.0 / CUTOFF)
+    left = 1.0 - scaled * scaled
+    inside = d < CUTOFF
+    values = [
+        jnp.full_like(x, SCALE),
+        (SCALE * S3) * x,
+        (SCALE * S3) * y,
+        (SCALE * S3) * z,
+        (SCALE * S15) * (x * y),
+        (SCALE * S15) * (y * z),
+        (SCALE * 0.5 * S5) * (3.0 * z * z - 1.0),
+        (SCALE * S15) * (x * z),
+        (SCALE * 0.5 * S15) * (x * x - y * y),
+        x,
+        y,
+        z,
+        inv,
+        jnp.where(inside, left * left, 0.0),
+        jnp.where(inside, (-4.0 / CUTOFF) * scaled * left, 0.0),
+    ]
+    for number, value in enumerate(values):
+        geo_d[number * DENSE : (number + 1) * DENSE, :] = value
+    sine, cosine = sin_cos(d * (math.pi / CUTOFF))
+    twice = 2.0 * cosine
+    sine_last, cosine_last = jnp.zeros_like(sine), jnp.ones_like(sine)
+    root = math.sqrt(2.0 / CUTOFF)
+    for number in range(8):
+        bessel = root * sine * inv
+        bes_d[number * DENSE : (number + 1) * DENSE, :] = bessel
+        slope_d[number * DENSE : (number + 1) * DENSE, :] = (
+            (root * (math.pi / CUTOFF) * (number + 1)) * cosine - bessel
+        ) * inv
+        sine, sine_last = twice * sine - sine_last, sine
+        cosine, cosine_last = twice * cosine - cosine_last, cosine
+
+    def radial_step(step):
+        basis = jnp.concatenate([get_eight(bes_d, step), get_eight(slope_d, step)], axis=1)
+        a, b, c = split3(basis)
+        zero = jnp.zeros_like(a)
+        stack = jnp.concatenate([a, b, a, b, c, a, zero, zero], axis=0).astype(BF16)
+        both = mm(w6[...], stack)
+        u, u_d = both[:, :TILE], both[:, TILE:]
+        gate = 1.0 / (1.0 + jnp.exp(-u))
+        hidden = u * gate
+        slope = gate + hidden * (1.0 - gate)
+        env, env_d = get_row(geo_d, 13, step), get_row(geo_d, 14, step)
+        g = jnp.concatenate([env * hidden, env_d * hidden + env * (slope * u_d)], axis=1)
+        hi, lo = split2(g)
+        radial = mm(w3[...], jnp.concatenate([hi, lo, hi], axis=0))
+        r_s[:, span(step)] = radial[:, :TILE]
+        rp_s[:, span(step)] = radial[:, TILE:]
+
+    loop(0, STEPS, radial_step, UNROLL_RADIAL)
+
+    def messages(step, signs, features):
+        radial = r_s[:, span(step)]
         for degree in range(3):
             product = radial[degree * CH : (degree + 1) * CH] * features
             for q in range(9):
                 if DEGREE[q] != degree:
                     continue
-                hi, lo = split2(shapes[q] * product)
-                m_s[q * CH : (q + 1) * CH, :] = hi
-                m_s[ROWS_PAD + q * CH : ROWS_PAD + (q + 1) * CH, :] = lo
-
-    def first_step(step, carry):
-        at = pl.ds(pl.multiple_of(step * TILE, TILE), TILE)
-        live = iota((1, TILE), 1) + step * TILE < count
-        got = mm(ext_l[...], oh2[:, at])
-        fb_s[:, at] = got[0:CH]
-        relative = unpack(got) - pa_s[:, at]
-        rx = jnp.where(live, relative[0:1], 2.0)
-        ry = jnp.where(live, relative[1:2], 0.0)
-        rz = jnp.where(live, relative[2:3], 0.0)
-        d = jnp.sqrt(rx * rx + ry * ry + rz * rz)
-        inv = 1.0 / d
-        x, y, z = rx * inv, ry * inv, rz * inv
-        scaled = d * (1.0 / CUTOFF)
-        left = 1.0 - scaled * scaled
-        inside = d < CUTOFF
-        env = jnp.where(inside, left * left, 0.0)
-        env_d = jnp.where(inside, (-4.0 / CUTOFF) * scaled * left, 0.0)
-        shapes = [
-            jnp.full_like(x, SCALE),
-            (SCALE * S3) * x,
-            (SCALE * S3) * y,
-            (SCALE * S3) * z,
-            (SCALE * S15) * (x * y),
-            (SCALE * S15) * (y * z),
-            (SCALE * 0.5 * S5) * (3.0 * z * z - 1.0),
-            (SCALE * S15) * (x * z),
-            (SCALE * 0.5 * S15) * (x * x - y * y),
-        ]
-        for number, value in enumerate(shapes + [x, y, z, inv]):
-            geo[number : number + 1, at] = value
-        order = (iota((8, TILE), 0) + 1).astype(F32)
-        sine, cosine = sin_cos(order * (d * (math.pi / CUTOFF)))
-        root = math.sqrt(2.0 / CUTOFF)
-        bessel = root * sine * inv
-        bessel_d = (root * (math.pi / CUTOFF) * order * cosine - bessel) * inv
-        both = mm(win_ref[...], jnp.concatenate([bessel, bessel_d], axis=1), precision=HIGHEST)
-        u, u_d = both[:, :TILE], both[:, TILE:]
-        gate = 1.0 / (1.0 + jnp.exp(-u))
-        hidden = u * gate
-        slope = gate * (1.0 + u * (1.0 - gate))
-        g = jnp.concatenate([env * hidden, env_d * hidden + env * (slope * u_d)], axis=1)
-        hi, lo = split2(g)
-        radial = mm(w3[...], jnp.concatenate([hi, lo, hi], axis=0))
-        r_s[:, at] = radial[:, :TILE]
-        rp_s[:, at] = radial[:, TILE:]
-        messages(
-            [PARITY[q] * shapes[q] for q in range(9)], radial[:, :TILE], fa_s[:, at]
-        )
-        out = mm(oh2[0:EXT, at], m_s[...], NT)
-        s2[...] += out[:, :ROWS] + out[:, ROWS_PAD : ROWS_PAD + ROWS]
-        return carry
-
-    lax.fori_loop(0, STEPS, first_step, 0)
+                shape = get_row(geo_d, q, step)
+                hi, lo = split2((shape * product) if signs[q] > 0 else (-shape * product))
+                m_s[q * CH : (q + 1) * CH, 0:TILE] = hi
+                m_s[q * CH : (q + 1) * CH, TILE : 2 * TILE] = lo
+
+    s2[...] = jnp.zeros_like(s2)
+
+    def other_step(step):
+        messages(step, PARITY, fa_s[:, span(step)])
+        table = oh2[0:EXT, span(step)]
+        s2[...] += mm(jnp.concatenate([table, table], axis=1), m_s[...], NT)
+
+    loop(0, STEPS, other_step, UNROLL_SUMS)
 
     c0 = push(4, s2.at[pl.ds(2 * OWN, GY)], rsy.at[pl.ds(GY, GY)], y_low)
     c1 = push(5, s2.at[pl.ds(2 * OWN + GY, GY)], rsy.at[pl.ds(0, GY)], y_high)
 
-    def second_step(step, carry):
-        at = pl.ds(pl.multiple_of(step * TILE, TILE), TILE)
-        messages([geo[q : q + 1, at] for q in range(9)], r_s[:, at], fb_s[:, at])
-        out = mm(oh1[:, at], m_s[...], NT)
-        s1[...] += out[:, :ROWS] + out[:, ROWS_PAD : ROWS_PAD + ROWS]
-        return carry
-
-    lax.fori_loop(0, STEPS // 2, second_step, 0)
+    s1[...] = jnp.zeros_like(s1)
+
+    def own_sum_step(step):
+        messages(step, (1.0,) * 9, fb_s[:, span(step)])
+        table = oh1[:, span(step)]
+        s1[...] += mm(m_s[...], jnp.concatenate([table, table], axis=1), NT)
+
+    loop(0, STEPS // 2, own_sum_step, UNROLL_SUMS)
     settle(c0, c1)
     if comm:
         hi, lo = split2(rsy[...])
         s2[0 : 2 * OWN, :] += mm(ohy_t[:, 0 : 2 * GY], hi) + mm(ohy_t[:, 0 : 2 * GY], lo)
     c0 = push(6, s2.at[pl.ds(OWN, GX)], rsx.at[pl.ds(GX, GX)], x_low)
     c1 = push(7, s2.at[pl.ds(OWN + GX, GX)], rsx.at[pl.ds(0, GX)], x_high)
-    lax.fori_loop(STEPS // 2, STEPS, second_step, 0)
-    settle(c0, c1)
-    sums_t = s2[0:OWN, :] + s1[...]
+    loop(STEPS // 2, STEPS, own_sum_step, UNROLL_SUMS)
+    settle(c0, c1)
+    sums_t = s2[0:OWN, :]
     if comm:
         hi, lo = split2(rsx[...])
         sums_t = sums_t + mm(ohx_t, hi) + mm(ohx_t, lo)
 
-    sums = sums_t.T
+    sums = s1[...] + sums_t.T
     squares = [sums[q * CH : (q + 1) * CH] * sums[q * CH : (q + 1) * CH] for q in range(9)]
     invariant = jnp.concatenate(
         [
@@ -374,34 +441,29 @@
         gext[:, start : start + count_here] = hi
         gext[:, EXT_PAD + start : EXT_PAD + start + count_here] = lo
 
-    def contract(step, gathered, features):
-        at = pl.ds(pl.multiple_of(step * TILE, TILE), TILE)
-        along = jnp.zeros((CH, TILE), F32)
-        rows_z = []
+    def contract(step, gathered, features, target):
+        along = None
         for degree in range(3):
-            radial = r_s[degree * CH : (degree + 1) * CH, at]
+            part = slice(degree * CH, (degree + 1) * CH)
+            radial = r_s[part, span(step)] * features
+            slope = rp_s[part, span(step)] * features
             total = None
             for q in range(9):
                 if DEGREE[q] != degree:
                     continue
-                product = gathered[q * CH : (q + 1) * CH] * features
-                rows_z.append(jnp.sum(radial * product, axis=0, keepdims=True))
-                term = geo[q : q + 1, at] * product
+                here = gathered[q * CH : (q + 1) * CH]
+                put_row(target, q, step, jnp.sum(radial * here, axis=0, keepdims=True))
+                term = get_row(geo_d, q, step) * here
                 total = term if total is None else total + term
-            along = along + rp_s[degree * CH : (degree + 1) * CH, at] * total
-        rows_z.append(jnp.sum(along, axis=0, keepdims=True))
-        return rows_z
-
-    def own_step(step, carry):
-        at = pl.ds(pl.multiple_of(step * TILE, TILE), TILE)
-        table = oh1[:, at]
+            along = slope * total if along is None else along + slope * total
+        put_row(target, 9, step, jnp.sum(along, axis=0, keepdims=True))
+
+    def own_step(step):
+        table = oh1[:, span(step)]
         gathered = mm(gown[...], jnp.concatenate([table, table], axis=0))
-        rows_z = contract(step, gathered, fb_s[:, at])
-        for number, value in enumerate(rows_z):
-            zacc[number : number + 1, at] = value
-        return carry
-
-    lax.fori_loop(0, 8, own_step, 0)
+        contract(step, gathered, fb_s[:, span(step)], z_own)
+
+    loop(0, 8, own_step, UNROLL_BACK)
     settle(c0, c1)
     if comm:
         hi, lo = split2(rgx[...])
@@ -411,51 +473,50 @@
     c1 = push(11, sgy.at[pl.ds(GY, GY)], rgy.at[pl.ds(0, GY)], y_high)
     if comm:
         store_ghosts(rgx[...], OWN)
-    lax.fori_loop(8, STEPS, own_step, 0)
+    loop(8, STEPS, own_step, UNROLL_BACK)
     settle(c0, c1)
     if comm:
         store_ghosts(rgy[...], 2 * OWN)
 
-    facc[...] = jnp.zeros_like(facc)
-
-    def last_step(step, carry):
-        at = pl.ds(pl.multiple_of(step * TILE, TILE), TILE)
-        table = oh2[:, at]
+    def ext_step(step):
+        table = oh2[:, span(step)]
         gathered = mm(gext[...], jnp.concatenate([table, table], axis=0))
-        rows_z = contract(step, gathered, fa_s[:, at])
-        z = [rows_z[q] + zacc[q : q + 1, at] for q in range(10)]
-        nx, ny, nz = geo[9:10, at], geo[10:11, at], geo[11:12, at]
-        inv = geo[12:13, at]
-        gx = S3 * z[1] + S15 * (ny * z[4] + nz * z[7] + nx * z[8])
-        gy = S3 * z[2] + S15 * (nx * z[4] + nz * z[5] - ny * z[8])
-        gz = S3 * z[3] + S15 * (ny * z[5] + nx * z[7]) + (3.0 * S5) * (nz * z[6])
-        factor = SCALE * inv
-        gx, gy, gz = gx * factor, gy * factor, gz * factor
-        radial_part = z[9] - (gx * nx + gy * ny + gz * nz)
-        zero = jnp.zeros((5, TILE), F32)
-        pulled = jnp.concatenate(
-            [gx + radial_part * nx, gy + radial_part * ny, gz + radial_part * nz, zero], axis=0
-        )
+        contract(step, gathered, fa_s[:, span(step)], z_ext)
+
+    loop(0, STEPS, ext_step, UNROLL_BACK)
+
+    zs = [dense(z_own, q) + dense(z_ext, q) for q in range(10)]
+    nx, ny, nz, inv = [dense(geo_d, number) for number in range(9, 13)]
+    factor = SCALE * inv
+    gx = factor * (S3 * zs[1] + S15 * (ny * zs[4] + nz * zs[7] + nx * zs[8]))
+    gy = factor * (S3 * zs[2] + S15 * (nx * zs[4] + nz * zs[5] - ny * zs[8]))
+    gz = factor * (S3 * zs[3] + S15 * (ny * zs[5] + nx * zs[7]) + (3.0 * S5) * (nz * zs[6]))
+    along = zs[9] - (gx * nx + gy * ny + gz * nz)
+    pull_d[...] = jnp.zeros_like(pull_d)
+    for number, value in enumerate([gx + along * nx, gy + along * ny, gz + along * nz]):
+        pull_d[number * DENSE : (number + 1) * DENSE, :] = value
+    for step in range(STEPS):
+        pulled = get_eight(pull_d, step)
         hi = pulled.astype(BF16).astype(F32)
-        pieces = jnp.concatenate([hi, pulled - hi], axis=0).astype(BF16)
-        facc[...] -= mm(table, pieces, NT)
-        facc[0:OWN, :] += mm(oh1[:, at], pieces, NT)
-        return carry
-
-    lax.fori_loop(0, STEPS, last_step, 0)
+        pieces_s[:, step * TILE : (step + 1) * TILE] = jnp.concatenate(
+            [hi, pulled - hi], axis=0
+        ).astype(BF16)
+    at_first = mm(oh1[...], pieces_s[...], NT)
+    at_second = mm(oh2[...], pieces_s[...], NT)
 
     def home(rows8, table):
         a, b, c = split3(rows8)
         out = mm(jnp.concatenate([a, b, c, jnp.zeros_like(a)], axis=0).astype(BF16), table)
         return out[0:8] + out[8:16] + out[16:24]
 
-    total = facc[...].T
-    total = total[0:8] + total[8:16]
+    at_first, at_second = at_first.T, -at_second.T
+    at_first = at_first[0:8] + at_first[8:16]
+    total = at_second[0:8] + at_second[8:16]
     send_f[0] = total[:, 2 * OWN : 3 * OWN]
     c0 = push(12, send_f.at[0], recv_f.at[1], y_low)
     c1 = push(13, send_f.at[0], recv_f.at[0], y_high)
     settle(c0, c1)
-    near = total[:, 0 : 2 * OWN]
+    near = jnp.concatenate([total[:, 0:OWN] + at_first, total[:, OWN : 2 * OWN]], axis=1)
     if comm:
         near = near + home(fold_y(recv_f[0], recv_f[1]), ohy)
     send_f[1] = near[:, OWN : 2 * OWN]
@@ -494,14 +555,19 @@
         pltpu.VMEM((4, CH + 8, OWN), F32),
         pltpu.VMEM((CH + 32, EXT_PAD), BF16),
         pltpu.VMEM((8, SLOTS), F32),
+        pltpu.VMEM((3 * DENSE, OWN), F32),
+        pltpu.VMEM((8 * DENSE, OWN), F32),
+        pltpu.VMEM((8 * DENSE, OWN), F32),
+        pltpu.VMEM((16 * DENSE, OWN), F32),
+        pltpu.VMEM((8 * DENSE, OWN), F32),
         pltpu.VMEM((CH, SLOTS), F32),
         pltpu.VMEM((CH, SLOTS), F32),
-        pltpu.VMEM((16, SLOTS), F32),
         pltpu.VMEM((3 * CH, SLOTS), F32),
         pltpu.VMEM((3 * CH, SLOTS), F32),
         pltpu.VMEM((3 * CH, 3 * CH), BF16),
-        pltpu.VMEM((2 * ROWS_PAD, TILE), BF16),
-        pltpu.VMEM((OWN, ROWS), F32),
+        pltpu.VMEM((CH, 64), BF16),
+        pltpu.VMEM((ROWS, 2 * TILE), BF16),
+        pltpu.VMEM((ROWS, OWN), F32),
         pltpu.VMEM((EXT, ROWS), F32),
         pltpu.VMEM((2 * GY, ROWS), F32),
         pltpu.VMEM((2 * GX, ROWS), F32),
@@ -511,8 +577,9 @@
         pltpu.VMEM((2 * GX, ROWS), F32),
         pltpu.VMEM((2 * GY, ROWS), F32),
         pltpu.VMEM((2 * GY, ROWS), F32),
-        pltpu.VMEM((16, SLOTS), F32),
-        pltpu.VMEM((EXT_PAD, 16), F32),
+        pltpu.VMEM((10 * DENSE, OWN), F32),
+        pltpu.VMEM((10 * DENSE, OWN), F32),
+        pltpu.VMEM((16, SLOTS), BF16),
         pltpu.VMEM((2, 8, OWN), F32),
         pltpu.VMEM((4, 8, OWN), F32),
         pltpu.SemaphoreType.DMA((16,)),
@@ -538,8 +605,8 @@
         edge_count,
         send_list_x.reshape(1, -1),
         send_list_y.reshape(1, -1),
-        radial_in,
-        radial_out,
+        radial_in.T,
+        radial_out.T,
         mix_weight,
         out_weight.reshape(1, -1),
         species_energy,

time: 86.8 us -> 79 us (0.910)
  Pallas kernels: 80.6 us -> 75.9 us
  local copies, waits for them, and re-layouts: 4.63 us -> 1.71 us
    pallas_call x1, Pallas kernels: 80.6 us -> 75.9 us  [run(): pl.pallas_call(functools.partial(body, comm, n_gx, n_gy), out_shape=(jax....]
    unnamed x10 -> x6, local copies, waits for them, and re-layouts: 4.63 us -> 1.71 us
where the time goes in v2:
time: 79 us; the launch traced here: 78.9 us
  Pallas kernels  75.9 us (96%)
  local copies, waits for them, and re-layouts  1.71 us (2%)
  between operations  1.3 us (2%)
    pallas_call x1, Pallas kernels, run(): pl.pallas_call(functools.partial(body, comm, n_gx, n_gy), out_shape=(jax....  75.9 us
    unnamed x6, local copies, waits for them, and re-layouts  1.71 us

profile of v2, /device:TPU:24, one launch (start us, length us, event | category | flops | bytes accessed | tf_op | source)
XLA Modules:
  0.0 78.9 jit_solution(1484579740035675873)
XLA Ops:
  1.3 75.9 %layer.1 = (f32[1,128]{1,0:T(1,128)}, f32[3,128]{1,0:T(4,128)}) custom-call(f32[3,128]{1,0:T(4,128)} %pos_ref.1, bf16[64,128]{1,0:T(8,128)(2,1)} %feat_ref.1, s32[1,128]{1,0:T(1,128)} %bitcast.9, s32[2,3584]{1,0:T(2,128)} %edge_ref.1, s32[1]{0:T(128)S(6)} %copy.16.cnt_ref, s32[1,128]{1,0:T(1,128)} %bitcast.10, s32[1,64]{1,0:T(1,128)} %bitcast.11, ...), custom_call_target="tpu_custom_call" | custom-call | tf_op jit(solution)/shard_map/layer/pallas_call | solution.py:589
  77.2 0.0 copy-start.1
  77.2 0.0 copy-start
  77.2 0.6 copy-done.1
  77.8 0.5 copy.17
  78.3 0.0 copy-done
  78.3 0.6 copy.18
Async XLA Ops:
  77.2 0.6 copy-start.1
  77.2 1.1 %copy-start = (f32[3,128]{1,0:T(4,128)S(1)}, f32[3,128]{1,0:T(4,128)}, u32[]{:S(2)}) copy-start(f32[3,128]{1,0:T(4,128)} %get-tuple-element.9) | copy-start | bytes 4612

commit v3 on v2

--- a/solution.py
+++ b/solution.py
@@ -33,10 +33,10 @@
 DEGREE = (0, 1, 1, 1, 2, 2, 2, 2, 2)
 PARITY = (1.0, -1.0, -1.0, -1.0, 1.0, 1.0, 1.0, 1.0, 1.0)
 
-UNROLL_GATHER = 1
-UNROLL_RADIAL = 1
-UNROLL_SUMS = 1
-UNROLL_BACK = 1
+UNROLL_GATHER = True
+UNROLL_RADIAL = True
+UNROLL_SUMS = True
+UNROLL_BACK = True
 
 NN = (((1,), (0,)), ((), ()))
 NT = (((1,), (1,)), ((), ()))

time: 79 us -> 71 us (0.90)
  Pallas kernels: 75.9 us -> 67.9 us
    pallas_call x1, Pallas kernels: 75.9 us -> 67.9 us  [run(): pl.pallas_call(functools.partial(body, comm, n_gx, n_gy), out_shape=(jax....]
where the time goes in v3:
time: 71 us; the launch traced here: 70.9 us
  Pallas kernels  67.9 us (96%)
  local copies, waits for them, and re-layouts  1.71 us (2%)
  between operations  1.31 us (2%)
    pallas_call x1, Pallas kernels, run(): pl.pallas_call(functools.partial(body, comm, n_gx, n_gy), out_shape=(jax....  67.9 us
    unnamed x6, local copies, waits for them, and re-layouts  1.71 us

profile of v3, /device:TPU:24, one launch (start us, length us, event | category | flops | bytes accessed | tf_op | source)
XLA Modules:
  0.0 70.9 jit_solution(1086279337890061415)
XLA Ops:
  1.3 67.9 %layer.1 = (f32[1,128]{1,0:T(1,128)}, f32[3,128]{1,0:T(4,128)}) custom-call(f32[3,128]{1,0:T(4,128)} %pos_ref.1, bf16[64,128]{1,0:T(8,128)(2,1)} %feat_ref.1, s32[1,128]{1,0:T(1,128)} %bitcast.9, s32[2,3584]{1,0:T(2,128)} %edge_ref.1, s32[1]{0:T(128)S(6)} %copy.16.cnt_ref, s32[1,128]{1,0:T(1,128)} %bitcast.10, s32[1,64]{1,0:T(1,128)} %bitcast.11, ...), custom_call_target="tpu_custom_call" | custom-call | tf_op jit(solution)/shard_map/layer/pallas_call | solution.py:589
  69.1 0.0 copy-start.1
  69.2 0.0 copy-start
  69.2 0.6 copy-done.1
  69.8 0.5 copy.17
  70.3 0.0 copy-done
  70.3 0.6 copy.18
Async XLA Ops:
  69.1 0.6 copy-start.1
  69.2 1.1 %copy-start = (f32[3,128]{1,0:T(4,128)S(1)}, f32[3,128]{1,0:T(4,128)}, u32[]{:S(2)}) copy-start(f32[3,128]{1,0:T(4,128)} %get-tuple-element.9) | copy-start | bytes 4612

commit v4 on v3

--- a/solution.py
+++ b/solution.py
@@ -31,6 +31,7 @@
 S5 = math.sqrt(5.0)
 S15 = math.sqrt(15.0)
 DEGREE = (0, 1, 1, 1, 2, 2, 2, 2, 2)
+GROUPS = (((2,), 256, 576), ((0, 1), 0, 256))
 PARITY = (1.0, -1.0, -1.0, -1.0, 1.0, 1.0, 1.0, 1.0, 1.0)
 
 UNROLL_GATHER = True
@@ -95,14 +96,15 @@
     mix_ref,
     outw_ref,
     se_ref,
-    energy_ref,
-    force_ref,
+    out_ref,
     pos8,
     slyp,
     oh1,
     oh2,
-    send_a,
-    recv_a,
+    send_x,
+    recv_x,
+    send_y,
+    recv_y,
     ext_l,
     pa_s,
     rel_d,
@@ -117,16 +119,25 @@
     w3,
     w6,
     m_s,
+    m2_s,
     s1,
-    s2,
-    rsy,
-    rsx,
+    s2a,
+    s2b,
+    rsya,
+    rsyb,
+    rsxa,
+    rsxb,
     gown,
+    gown2,
     gext,
-    sgx,
-    rgx,
-    sgy,
-    rgy,
+    sgxa,
+    sgxb,
+    rgxa,
+    rgxb,
+    sgya,
+    sgyb,
+    rgya,
+    rgyb,
     z_own,
     z_ext,
     pieces_s,
@@ -135,6 +146,8 @@
     send_sem,
     recv_sem,
 ):
+    s2, rsy, rsx = (s2a, s2b), (rsya, rsyb), (rsxa, rsxb)
+    sgx, rgx, sgy, rgy = (sgxa, sgxb), (rgxa, rgxb), (sgya, sgyb), (rgya, rgyb)
     if comm:
         ix = lax.axis_index("gx")
         iy = lax.axis_index("gy")
@@ -198,12 +211,18 @@
     own_l = pack(jnp.concatenate([feat_ref[...].astype(F32), pos8[...]], axis=0))
     ext_l[:, 0:OWN] = own_l
     picked = mm(own_l, ohx_t)
-    send_a[0, 0:CH, :] = picked[0:CH]
-    send_a[0, CH : CH + 8, :] = unpack(picked)
+    half = CH // 2
+    upper, lower = picked[0:half], picked[half:CH]
+    near_low = lane < GX
+    send_x[0, 0:half, :] = jnp.where(near_low, upper, pltpu.roll(lower, GX, 1))
+    send_x[1, 0:half, :] = jnp.where(near_low, pltpu.roll(upper, GX, 1), lower)
+    coordinates = unpack(picked)
+    send_x[0, half:, :] = coordinates
+    send_x[1, half:, :] = coordinates
     if comm:
         pl.semaphore_wait(barrier, 4)
-    c0 = push(0, send_a.at[0], recv_a.at[1], x_low)
-    c1 = push(1, send_a.at[0], recv_a.at[0], x_high)
+    c0 = push(0, send_x.at[0], recv_x.at[1], x_low)
+    c1 = push(1, send_x.at[1], recv_x.at[0], x_high)
 
     hi, lo = split2(wout_ref[...])
     hi, lo = hi.astype(F32), lo.astype(F32)
@@ -230,18 +249,23 @@
 
     settle(c0, c1)
     if comm:
-        section = pack(fold_x(recv_a[0], recv_a[1]))
+        low, high = recv_x[0], recv_x[1]
+        turned_low, turned_high = pltpu.roll(low, GX, 1), pltpu.roll(high, GX, 1)
+        upper = jnp.where(near_low, low[0:half], turned_high[0:half])
+        lower = jnp.where(near_low, turned_low[0:half], high[0:half])
+        coordinates = jnp.where(near_low, turned_low[half:], turned_high[half:])
+        section = pack(jnp.concatenate([upper, lower, coordinates], axis=0))
     else:
         section = own_l
     ext_l[:, OWN : 2 * OWN] = section
     picked = mm(own_l, ohy_t[0:OWN]) + mm(section, ohy_t[OWN : 2 * OWN])
-    send_a[1, 0:CH, :] = picked[0:CH]
-    send_a[1, CH : CH + 8, :] = unpack(picked)
-    c0 = push(2, send_a.at[1], recv_a.at[3], y_low)
-    c1 = push(3, send_a.at[1], recv_a.at[2], y_high)
+    send_y[0:CH, :] = picked[0:CH]
+    send_y[CH : CH + 8, :] = unpack(picked)
+    c0 = push(2, send_y, recv_y.at[1], y_low)
+    c1 = push(3, send_y, recv_y.at[0], y_high)
     settle(c0, c1)
     if comm:
-        ext_l[:, 2 * OWN : 3 * OWN] = pack(fold_y(recv_a[2], recv_a[3]))
+        ext_l[:, 2 * OWN : 3 * OWN] = pack(fold_y(recv_y[0], recv_y[1]))
     else:
         ext_l[:, 2 * OWN : 3 * OWN] = jnp.where(lane < 2 * GY, own_l, 0.0)
 
@@ -349,52 +373,98 @@
 
     loop(0, STEPS, radial_step, UNROLL_RADIAL)
 
-    def messages(step, signs, features):
+    def messages(target, step, signs, features, degrees):
         radial = r_s[:, span(step)]
-        for degree in range(3):
+        for degree in degrees:
             product = radial[degree * CH : (degree + 1) * CH] * features
             for q in range(9):
                 if DEGREE[q] != degree:
                     continue
                 shape = get_row(geo_d, q, step)
                 hi, lo = split2((shape * product) if signs[q] > 0 else (-shape * product))
-                m_s[q * CH : (q + 1) * CH, 0:TILE] = hi
-                m_s[q * CH : (q + 1) * CH, TILE : 2 * TILE] = lo
-
-    s2[...] = jnp.zeros_like(s2)
-
-    def other_step(step):
-        messages(step, PARITY, fa_s[:, span(step)])
-        table = oh2[0:EXT, span(step)]
-        s2[...] += mm(jnp.concatenate([table, table], axis=1), m_s[...], NT)
-
-    loop(0, STEPS, other_step, UNROLL_SUMS)
-
-    c0 = push(4, s2.at[pl.ds(2 * OWN, GY)], rsy.at[pl.ds(GY, GY)], y_low)
-    c1 = push(5, s2.at[pl.ds(2 * OWN + GY, GY)], rsy.at[pl.ds(0, GY)], y_high)
+                target[q * CH : (q + 1) * CH, 0:TILE] = hi
+                target[q * CH : (q + 1) * CH, TILE : 2 * TILE] = lo
+
+    s2a[...] = jnp.zeros_like(s2a)
+    s2b[...] = jnp.zeros_like(s2b)
+
+    def other_step(group):
+        degrees, start, stop = GROUPS[group]
+
+        def one(step):
+            messages(m_s, step, PARITY, fa_s[:, span(step)], degrees)
+            table = oh2[OWN:EXT, span(step)]
+            table = jnp.concatenate([table, table], axis=1)
+            s2[group][...] += mm(table, m_s[start:stop, :], NT)
+
+        return one
+
+    def push_sums_y(group):
+        base = 4 + 2 * group
+        src, dst = s2[group], rsy[group]
+        return (
+            push(base, src.at[pl.ds(OWN, GY)], dst.at[pl.ds(GY, GY)], y_low),
+            push(base + 1, src.at[pl.ds(OWN + GY, GY)], dst.at[pl.ds(0, GY)], y_high),
+        )
+
+    def push_sums_x(group):
+        base = 8 + 2 * group
+        src, dst = s2[group], rsx[group]
+        return (
+            push(base, src.at[pl.ds(0, GX)], dst.at[pl.ds(GX, GX)], x_low),
+            push(base + 1, src.at[pl.ds(GX, GX)], dst.at[pl.ds(0, GX)], x_high),
+        )
+
+    def add_sums_y(group):
+        if comm:
+            hi, lo = split2(rsy[group][...])
+            table = ohy_t[OWN : 2 * OWN, 0 : 2 * GY]
+            s2[group][0:OWN, :] += mm(table, hi) + mm(table, lo)
 
     s1[...] = jnp.zeros_like(s1)
 
     def own_sum_step(step):
-        messages(step, (1.0,) * 9, fb_s[:, span(step)])
-        table = oh1[:, span(step)]
-        s1[...] += mm(m_s[...], jnp.concatenate([table, table], axis=1), NT)
-
+        messages(m_s, step, (1.0,) * 9, fb_s[:, span(step)], (0, 1, 2))
+        messages(m2_s, step, PARITY, fa_s[:, span(step)], (0, 1, 2))
+        table1, table2 = oh1[:, span(step)], oh2[0:OWN, span(step)]
+        s1[...] += mm(m_s[...], jnp.concatenate([table1, table1], axis=1), NT) + mm(
+            m2_s[...], jnp.concatenate([table2, table2], axis=1), NT
+        )
+
+    other_step_a, other_step_b = other_step(0), other_step(1)
+    loop(0, STEPS, other_step_a, UNROLL_SUMS)
+    y_a = push_sums_y(0)
+    loop(0, STEPS, other_step_b, UNROLL_SUMS)
+    y_b = push_sums_y(1)
     loop(0, STEPS // 2, own_sum_step, UNROLL_SUMS)
-    settle(c0, c1)
-    if comm:
-        hi, lo = split2(rsy[...])
-        s2[0 : 2 * OWN, :] += mm(ohy_t[:, 0 : 2 * GY], hi) + mm(ohy_t[:, 0 : 2 * GY], lo)
-    c0 = push(6, s2.at[pl.ds(OWN, GX)], rsx.at[pl.ds(GX, GX)], x_low)
-    c1 = push(7, s2.at[pl.ds(OWN + GX, GX)], rsx.at[pl.ds(0, GX)], x_high)
+    settle(*y_a)
+    add_sums_y(0)
+    x_a = push_sums_x(0)
     loop(STEPS // 2, STEPS, own_sum_step, UNROLL_SUMS)
-    settle(c0, c1)
-    sums_t = s2[0:OWN, :]
-    if comm:
-        hi, lo = split2(rsx[...])
-        sums_t = sums_t + mm(ohx_t, hi) + mm(ohx_t, lo)
-
-    sums = s1[...] + sums_t.T
+    settle(*y_b)
+    add_sums_y(1)
+    x_b = push_sums_x(1)
+
+    def home_sums(group):
+        _, start, stop = GROUPS[group]
+        total = s1[start:stop, :]
+        if comm:
+            hi, lo = split2(rsx[group][...])
+            total = total + (home_y[group] + mm(ohx_t, hi) + mm(ohx_t, lo)).T
+        return total
+
+    home_y = []
+    for group in range(2):
+        hi, lo = split2(rsy[group][...])
+        table = ohy_t[0:OWN, 0 : 2 * GY]
+        home_y.append(mm(table, hi) + mm(table, lo))
+
+    settle(*x_a)
+    sums_a = home_sums(0)
+    settle(*x_b)
+    sums_b = home_sums(1)
+
+    sums = jnp.concatenate([sums_b, sums_a], axis=0)
     squares = [sums[q * CH : (q + 1) * CH] * sums[q * CH : (q + 1) * CH] for q in range(9)]
     invariant = jnp.concatenate(
         [
@@ -413,7 +483,7 @@
     shift = jnp.zeros_like(energy)
     for k in range(5):
         shift = jnp.where(kind == k, se_ref[k], shift)
-    energy_ref[...] = energy + shift
+    out_ref[3:4, :] = energy + shift
     d_mixed = weight * (gate * (1.0 + mixed * (1.0 - gate)))
     d_inv = 2.0 * mm(mix_ref[...].T, d_mixed, precision=HIGHEST)
     gext[...] = jnp.zeros_like(gext)
@@ -424,68 +494,106 @@
         gown[at, 0:OWN] = hi
         gown[at, OWN : 2 * OWN] = lo
         hi, lo = split2(PARITY[q] * gradient)
-        gext[at, 0:OWN] = hi
-        gext[at, EXT_PAD : EXT_PAD + OWN] = lo
-
-    def own_rows(table):
-        return mm(table, gext[:, 0:OWN], NT) + mm(table, gext[:, EXT_PAD : EXT_PAD + OWN], NT)
-
-    sgx[...] = own_rows(ohx)
-    c0 = push(8, sgx.at[pl.ds(0, GX)], rgx.at[pl.ds(GX, GX)], x_low)
-    c1 = push(9, sgx.at[pl.ds(GX, GX)], rgx.at[pl.ds(0, GX)], x_high)
-    outgoing_y = own_rows(ohy[0 : 2 * GY, 0:OWN])
-
-    def store_ghosts(rows, start):
-        hi, lo = split2(rows.T)
-        count_here = rows.shape[0]
-        gext[:, start : start + count_here] = hi
-        gext[:, EXT_PAD + start : EXT_PAD + start + count_here] = lo
-
-    def contract(step, gathered, features, target):
+        gown2[at, 0:OWN] = hi
+        gown2[at, OWN : 2 * OWN] = lo
+
+    def own_rows(table, group):
+        _, start, stop = GROUPS[group]
+        return mm(table, gown2[start:stop, 0:OWN], NT) + mm(
+            table, gown2[start:stop, OWN : 2 * OWN], NT
+        )
+
+    def push_gradient_x(group):
+        base = 12 + 2 * group
+        src, dst = sgx[group], rgx[group]
+        src[...] = own_rows(ohx, group)
+        return (
+            push(base, src.at[pl.ds(0, GX)], dst.at[pl.ds(GX, GX)], x_low),
+            push(base + 1, src.at[pl.ds(GX, GX)], dst.at[pl.ds(0, GX)], x_high),
+        )
+
+    def push_gradient_y(group, outgoing):
+        base = 16 + 2 * group
+        src, dst = sgy[group], rgy[group]
+        if comm:
+            hi, lo = split2(rgx[group][...])
+            table = ohy[0 : 2 * GY, OWN : 2 * OWN]
+            outgoing = outgoing + mm(table, hi) + mm(table, lo)
+        src[...] = outgoing
+        return (
+            push(base, src.at[pl.ds(0, GY)], dst.at[pl.ds(GY, GY)], y_low),
+            push(base + 1, src.at[pl.ds(GY, GY)], dst.at[pl.ds(0, GY)], y_high),
+        )
+
+    def store_ghosts(group, ref, start):
+        if comm:
+            _, first, last = GROUPS[group]
+            hi, lo = split2(ref[...].T)
+            width = ref.shape[0]
+            gext[first:last, start : start + width] = hi
+            gext[first:last, 2 * OWN + start : 2 * OWN + start + width] = lo
+
+    x_a = push_gradient_x(0)
+    x_b = push_gradient_x(1)
+    outgoing_a = own_rows(ohy[0 : 2 * GY, 0:OWN], 0)
+    outgoing_b = own_rows(ohy[0 : 2 * GY, 0:OWN], 1)
+
+    def contract(step, terms, first_row, target, degrees, last):
         along = None
-        for degree in range(3):
+        for degree in degrees:
             part = slice(degree * CH, (degree + 1) * CH)
-            radial = r_s[part, span(step)] * features
-            slope = rp_s[part, span(step)] * features
+            radial, slope = r_s[part, span(step)], rp_s[part, span(step)]
             total = None
             for q in range(9):
                 if DEGREE[q] != degree:
                     continue
-                here = gathered[q * CH : (q + 1) * CH]
+                rows = slice(q * CH - first_row, (q + 1) * CH - first_row)
+                here = None
+                for gathered, features in terms:
+                    product = gathered[rows] * features
+                    here = product if here is None else here + product
                 put_row(target, q, step, jnp.sum(radial * here, axis=0, keepdims=True))
                 term = get_row(geo_d, q, step) * here
                 total = term if total is None else total + term
             along = slope * total if along is None else along + slope * total
-        put_row(target, 9, step, jnp.sum(along, axis=0, keepdims=True))
+        put_row(target, last, step, jnp.sum(along, axis=0, keepdims=True))
 
     def own_step(step):
-        table = oh1[:, span(step)]
-        gathered = mm(gown[...], jnp.concatenate([table, table], axis=0))
-        contract(step, gathered, fb_s[:, span(step)], z_own)
-
-    loop(0, 8, own_step, UNROLL_BACK)
-    settle(c0, c1)
-    if comm:
-        hi, lo = split2(rgx[...])
-        table = ohy[0 : 2 * GY, OWN : 2 * OWN]
-        sgy[...] = outgoing_y + mm(table, hi) + mm(table, lo)
-    c0 = push(10, sgy.at[pl.ds(0, GY)], rgy.at[pl.ds(GY, GY)], y_low)
-    c1 = push(11, sgy.at[pl.ds(GY, GY)], rgy.at[pl.ds(0, GY)], y_high)
-    if comm:
-        store_ghosts(rgx[...], OWN)
-    loop(8, STEPS, own_step, UNROLL_BACK)
-    settle(c0, c1)
-    if comm:
-        store_ghosts(rgy[...], 2 * OWN)
-
-    def ext_step(step):
-        table = oh2[:, span(step)]
-        gathered = mm(gext[...], jnp.concatenate([table, table], axis=0))
-        contract(step, gathered, fa_s[:, span(step)], z_ext)
-
-    loop(0, STEPS, ext_step, UNROLL_BACK)
+        table1, table2 = oh1[:, span(step)], oh2[0:OWN, span(step)]
+        first = mm(gown[...], jnp.concatenate([table1, table1], axis=0))
+        second = mm(gown2[...], jnp.concatenate([table2, table2], axis=0))
+        terms = ((first, fb_s[:, span(step)]), (second, fa_s[:, span(step)]))
+        contract(step, terms, 0, z_own, (0, 1, 2), 9)
+
+    loop(0, STEPS, own_step, UNROLL_BACK)
+    settle(*x_a)
+    y_a = push_gradient_y(0, outgoing_a)
+    store_ghosts(0, rgxa, 0)
+    settle(*x_b)
+    y_b = push_gradient_y(1, outgoing_b)
+    store_ghosts(1, rgxb, 0)
+
+    def ext_step(group):
+        degrees, first, last = GROUPS[group]
+
+        def one(step):
+            table = oh2[OWN:EXT_PAD, span(step)]
+            gathered = mm(gext[first:last, :], jnp.concatenate([table, table], axis=0))
+            terms = ((gathered, fa_s[:, span(step)]),)
+            contract(step, terms, first, z_ext, degrees, 9 + group)
+
+        return one
+
+    ext_step_a, ext_step_b = ext_step(0), ext_step(1)
+    settle(*y_a)
+    store_ghosts(0, rgya, OWN)
+    loop(0, STEPS, ext_step_a, UNROLL_BACK)
+    settle(*y_b)
+    store_ghosts(1, rgyb, OWN)
+    loop(0, STEPS, ext_step_b, UNROLL_BACK)
 
     zs = [dense(z_own, q) + dense(z_ext, q) for q in range(10)]
+    zs[9] = zs[9] + dense(z_ext, 10)
     nx, ny, nz, inv = [dense(geo_d, number) for number in range(9, 13)]
     factor = SCALE * inv
     gx = factor * (S3 * zs[1] + S15 * (ny * zs[4] + nz * zs[7] + nx * zs[8]))
@@ -513,20 +621,20 @@
     at_first = at_first[0:8] + at_first[8:16]
     total = at_second[0:8] + at_second[8:16]
     send_f[0] = total[:, 2 * OWN : 3 * OWN]
-    c0 = push(12, send_f.at[0], recv_f.at[1], y_low)
-    c1 = push(13, send_f.at[0], recv_f.at[0], y_high)
+    c0 = push(20, send_f.at[0], recv_f.at[1], y_low)
+    c1 = push(21, send_f.at[0], recv_f.at[0], y_high)
     settle(c0, c1)
     near = jnp.concatenate([total[:, 0:OWN] + at_first, total[:, OWN : 2 * OWN]], axis=1)
     if comm:
         near = near + home(fold_y(recv_f[0], recv_f[1]), ohy)
     send_f[1] = near[:, OWN : 2 * OWN]
-    c0 = push(14, send_f.at[1], recv_f.at[3], x_low)
-    c1 = push(15, send_f.at[1], recv_f.at[2], x_high)
+    c0 = push(22, send_f.at[1], recv_f.at[3], x_low)
+    c1 = push(23, send_f.at[1], recv_f.at[2], x_high)
     settle(c0, c1)
     own = near[:, 0:OWN]
     if comm:
         own = own + home(fold_x(recv_f[2], recv_f[3]), ohx)
-    force_ref[...] = own[0:3]
+    out_ref[0:3, :] = own[0:3]
 
 
 def run(args, n_gx, n_gy, comm=True):
@@ -551,8 +659,10 @@
         pltpu.VMEM((1, OWN), jnp.int32),
         pltpu.VMEM((OWN, SLOTS), BF16),
         pltpu.VMEM((EXT_PAD, SLOTS), BF16),
+        pltpu.VMEM((2, CH // 2 + 8, OWN), F32),
+        pltpu.VMEM((2, CH // 2 + 8, OWN), F32),
+        pltpu.VMEM((CH + 8, OWN), F32),
         pltpu.VMEM((2, CH + 8, OWN), F32),
-        pltpu.VMEM((4, CH + 8, OWN), F32),
         pltpu.VMEM((CH + 32, EXT_PAD), BF16),
         pltpu.VMEM((8, SLOTS), F32),
         pltpu.VMEM((3 * DENSE, OWN), F32),
@@ -567,33 +677,39 @@
         pltpu.VMEM((3 * CH, 3 * CH), BF16),
         pltpu.VMEM((CH, 64), BF16),
         pltpu.VMEM((ROWS, 2 * TILE), BF16),
+        pltpu.VMEM((ROWS, 2 * TILE), BF16),
         pltpu.VMEM((ROWS, OWN), F32),
-        pltpu.VMEM((EXT, ROWS), F32),
-        pltpu.VMEM((2 * GY, ROWS), F32),
-        pltpu.VMEM((2 * GX, ROWS), F32),
+        pltpu.VMEM((EXT - OWN, 5 * CH), F32),
+        pltpu.VMEM((EXT - OWN, 4 * CH), F32),
+        pltpu.VMEM((2 * GY, 5 * CH), F32),
+        pltpu.VMEM((2 * GY, 4 * CH), F32),
+        pltpu.VMEM((2 * GX, 5 * CH), F32),
+        pltpu.VMEM((2 * GX, 4 * CH), F32),
         pltpu.VMEM((ROWS, 2 * OWN), BF16),
-        pltpu.VMEM((ROWS, 2 * EXT_PAD), BF16),
-        pltpu.VMEM((2 * GX, ROWS), F32),
-        pltpu.VMEM((2 * GX, ROWS), F32),
-        pltpu.VMEM((2 * GY, ROWS), F32),
-        pltpu.VMEM((2 * GY, ROWS), F32),
+        pltpu.VMEM((ROWS, 2 * OWN), BF16),
+        pltpu.VMEM((ROWS, 4 * OWN), BF16),
+        pltpu.VMEM((2 * GX, 5 * CH), F32),
+        pltpu.VMEM((2 * GX, 4 * CH), F32),
+        pltpu.VMEM((2 * GX, 5 * CH), F32),
+        pltpu.VMEM((2 * GX, 4 * CH), F32),
+        pltpu.VMEM((2 * GY, 5 * CH), F32),
+        pltpu.VMEM((2 * GY, 4 * CH), F32),
+        pltpu.VMEM((2 * GY, 5 * CH), F32),
+        pltpu.VMEM((2 * GY, 4 * CH), F32),
         pltpu.VMEM((10 * DENSE, OWN), F32),
-        pltpu.VMEM((10 * DENSE, OWN), F32),
+        pltpu.VMEM((11 * DENSE, OWN), F32),
         pltpu.VMEM((16, SLOTS), BF16),
         pltpu.VMEM((2, 8, OWN), F32),
         pltpu.VMEM((4, 8, OWN), F32),
-        pltpu.SemaphoreType.DMA((16,)),
-        pltpu.SemaphoreType.DMA((16,)),
+        pltpu.SemaphoreType.DMA((24,)),
+        pltpu.SemaphoreType.DMA((24,)),
     ]
     params = {"collective_id": 0, "has_side_effects": True} if comm else {}
-    energies, forces = pl.pallas_call(
+    both = pl.pallas_call(
         functools.partial(body, comm, n_gx, n_gy),
-        out_shape=(
-            jax.ShapeDtypeStruct((1, OWN), F32),
-            jax.ShapeDtypeStruct((3, OWN), F32),
-        ),
+        out_shape=jax.ShapeDtypeStruct((4, OWN), F32),
         in_specs=[vmem, vmem, vmem, vmem, smem, vmem, vmem, vmem, vmem, vmem, vmem, smem],
-        out_specs=(vmem, vmem),
+        out_specs=vmem,
         scratch_shapes=scratch,
         compiler_params=pltpu.CompilerParams(vmem_limit_bytes=60 * 1024 * 1024, **params),
         name="layer",
@@ -611,7 +727,7 @@
         out_weight.reshape(1, -1),
         species_energy,
     )
-    return energies.reshape(-1), forces
+    return both[3], both[0:3]
 
 
 def solution(mesh):

time: 71 us -> 68.1 us (0.959)
  Pallas kernels: 67.9 us -> 64.9 us
    pallas_call x1, Pallas kernels: 67.9 us -> 64.9 us  [run(): pl.pallas_call(functools.partial(body, comm, n_gx, n_gy), out_shape=jax.S...]
    squeeze x0 -> x1, local copies, waits for them, and re-layouts: none -> 1.25 us  [run(): return (both[3], both[0:3])]
    unnamed x6 -> x3, local copies, waits for them, and re-layouts: 1.71 us -> 0.58 us
where the time goes in v4:
time: 68.1 us; the launch traced here: 68 us
  Pallas kernels  64.9 us (95%)
  local copies, waits for them, and re-layouts  1.83 us (3%)
  between operations  1.3 us (2%)
    pallas_call x1, Pallas kernels, run(): pl.pallas_call(functools.partial(body, comm, n_gx, n_gy), out_shape=jax.S...  64.9 us

profile of v4, /device:TPU:24, one launch (start us, length us, event | category | flops | bytes accessed | tf_op | source)
XLA Modules:
  0.0 68.0 jit_solution(535894512697183825)
XLA Ops:
  1.3 64.9 %layer.1 = f32[4,128]{1,0:T(4,128)} custom-call(f32[3,128]{1,0:T(4,128)} %pos_ref.1, bf16[64,128]{1,0:T(8,128)(2,1)} %feat_ref.1, s32[1,128]{1,0:T(1,128)} %bitcast.12, s32[2,3584]{1,0:T(2,128)} %edge_ref.1, s32[1]{0:T(128)S(6)} %copy.15.cnt_ref, s32[1,128]{1,0:T(1,128)} %bitcast.13, s32[1,64]{1,0:T(1,128)} %bitcast.14, f32[8,64]{1,0:T(8,128)} %bitcast.11, ...), custom_call_target="tpu_custom_call" | custom-call | tf_op jit(solution)/shard_map/layer/pallas_call | solution.py:708
  66.1 0.0 copy-start
  66.2 1.2 %slice_bitcast_fusion = f32[128]{0:T(128)} fusion(f32[4,128]{1,0:T(4,128)} %layer.1), kind=kLoop, calls=%fused_computation | loop fusion | bytes 1024 | tf_op jit(solution)/shard_map/squeeze | solution.py:730
  67.4 0.0 copy-done
  67.4 0.6 copy.16
Async XLA Ops:
  66.1 1.3 %copy-start = (f32[4,128]{1,0:T(4,128)S(1)}, f32[4,128]{1,0:T(4,128)}, u32[]{:S(2)}) copy-start(f32[4,128]{1,0:T(4,128)} %layer.1) | copy-start | bytes 6148

commit v5 on v4

--- a/solution.py
+++ b/solution.py
@@ -96,7 +96,8 @@
     mix_ref,
     outw_ref,
     se_ref,
-    out_ref,
+    energy_ref,
+    force_ref,
     pos8,
     slyp,
     oh1,
@@ -119,7 +120,6 @@
     w3,
     w6,
     m_s,
-    m2_s,
     s1,
     s2a,
     s2b,
@@ -278,6 +278,14 @@
             return carry
 
         lax.fori_loop(start, stop, one, 0, unroll=unroll)
+
+    def ahead(start, stop, fetch, use, unroll):
+        def one(step, value):
+            following = fetch(jnp.minimum(step + 1, stop - 1))
+            use(step, value)
+            return following
+
+        lax.fori_loop(start, stop, one, fetch(start), unroll=unroll)
 
     def halves(value):
         return value[:, 0:OWN], value[:, OWN:TILE]
@@ -354,12 +362,14 @@
         sine, sine_last = twice * sine - sine_last, sine
         cosine, cosine_last = twice * cosine - cosine_last, cosine
 
-    def radial_step(step):
+    def radial_fetch(step):
         basis = jnp.concatenate([get_eight(bes_d, step), get_eight(slope_d, step)], axis=1)
         a, b, c = split3(basis)
         zero = jnp.zeros_like(a)
         stack = jnp.concatenate([a, b, a, b, c, a, zero, zero], axis=0).astype(BF16)
-        both = mm(w6[...], stack)
+        return mm(w6[...], stack)
+
+    def radial_use(step, both):
         u, u_d = both[:, :TILE], both[:, TILE:]
         gate = 1.0 / (1.0 + jnp.exp(-u))
         hidden = u * gate
@@ -371,7 +381,7 @@
         r_s[:, span(step)] = radial[:, :TILE]
         rp_s[:, span(step)] = radial[:, TILE:]
 
-    loop(0, STEPS, radial_step, UNROLL_RADIAL)
+    ahead(0, STEPS, radial_fetch, radial_use, UNROLL_RADIAL)
 
     def messages(target, step, signs, features, degrees):
         radial = r_s[:, span(step)]
@@ -392,10 +402,11 @@
         degrees, start, stop = GROUPS[group]
 
         def one(step):
-            messages(m_s, step, PARITY, fa_s[:, span(step)], degrees)
+            buffer = m_s.at[lax.rem(step, 2)]
+            messages(buffer, step, PARITY, fa_s[:, span(step)], degrees)
             table = oh2[OWN:EXT, span(step)]
             table = jnp.concatenate([table, table], axis=1)
-            s2[group][...] += mm(table, m_s[start:stop, :], NT)
+            s2[group][...] += mm(table, buffer[start:stop, :], NT)
 
         return one
 
@@ -424,11 +435,11 @@
     s1[...] = jnp.zeros_like(s1)
 
     def own_sum_step(step):
-        messages(m_s, step, (1.0,) * 9, fb_s[:, span(step)], (0, 1, 2))
-        messages(m2_s, step, PARITY, fa_s[:, span(step)], (0, 1, 2))
+        messages(m_s.at[0], step, (1.0,) * 9, fb_s[:, span(step)], (0, 1, 2))
+        messages(m_s.at[1], step, PARITY, fa_s[:, span(step)], (0, 1, 2))
         table1, table2 = oh1[:, span(step)], oh2[0:OWN, span(step)]
-        s1[...] += mm(m_s[...], jnp.concatenate([table1, table1], axis=1), NT) + mm(
-            m2_s[...], jnp.concatenate([table2, table2], axis=1), NT
+        s1[...] += mm(m_s[0], jnp.concatenate([table1, table1], axis=1), NT) + mm(
+            m_s[1], jnp.concatenate([table2, table2], axis=1), NT
         )
 
     other_step_a, other_step_b = other_step(0), other_step(1)
@@ -483,7 +494,7 @@
     shift = jnp.zeros_like(energy)
     for k in range(5):
         shift = jnp.where(kind == k, se_ref[k], shift)
-    out_ref[3:4, :] = energy + shift
+    energy_ref[...] = energy + shift
     d_mixed = weight * (gate * (1.0 + mixed * (1.0 - gate)))
     d_inv = 2.0 * mm(mix_ref[...].T, d_mixed, precision=HIGHEST)
     gext[...] = jnp.zeros_like(gext)
@@ -576,21 +587,23 @@
     def ext_step(group):
         degrees, first, last = GROUPS[group]
 
-        def one(step):
+        def fetch(step):
             table = oh2[OWN:EXT_PAD, span(step)]
-            gathered = mm(gext[first:last, :], jnp.concatenate([table, table], axis=0))
+            return mm(gext[first:last, :], jnp.concatenate([table, table], axis=0))
+
+        def use(step, gathered):
             terms = ((gathered, fa_s[:, span(step)]),)
             contract(step, terms, first, z_ext, degrees, 9 + group)
 
-        return one
-
-    ext_step_a, ext_step_b = ext_step(0), ext_step(1)
+        return fetch, use
+
+    ext_a, ext_b = ext_step(0), ext_step(1)
     settle(*y_a)
     store_ghosts(0, rgya, OWN)
-    loop(0, STEPS, ext_step_a, UNROLL_BACK)
+    ahead(0, STEPS, *ext_a, UNROLL_BACK)
     settle(*y_b)
     store_ghosts(1, rgyb, OWN)
-    loop(0, STEPS, ext_step_b, UNROLL_BACK)
+    ahead(0, STEPS, *ext_b, UNROLL_BACK)
 
     zs = [dense(z_own, q) + dense(z_ext, q) for q in range(10)]
     zs[9] = zs[9] + dense(z_ext, 10)
@@ -634,7 +647,7 @@
     own = near[:, 0:OWN]
     if comm:
         own = own + home(fold_x(recv_f[2], recv_f[3]), ohx)
-    out_ref[0:3, :] = own[0:3]
+    force_ref[...] = own[0:3]
 
 
 def run(args, n_gx, n_gy, comm=True):
@@ -676,8 +689,7 @@
         pltpu.VMEM((3 * CH, SLOTS), F32),
         pltpu.VMEM((3 * CH, 3 * CH), BF16),
         pltpu.VMEM((CH, 64), BF16),
-        pltpu.VMEM((ROWS, 2 * TILE), BF16),
-        pltpu.VMEM((ROWS, 2 * TILE), BF16),
+        pltpu.VMEM((2, ROWS, 2 * TILE), BF16),
         pltpu.VMEM((ROWS, OWN), F32),
         pltpu.VMEM((EXT - OWN, 5 * CH), F32),
         pltpu.VMEM((EXT - OWN, 4 * CH), F32),
@@ -705,11 +717,14 @@
         pltpu.SemaphoreType.DMA((24,)),
     ]
     params = {"collective_id": 0, "has_side_effects": True} if comm else {}
-    both = pl.pallas_call(
+    energies, forces = pl.pallas_call(
         functools.partial(body, comm, n_gx, n_gy),
-        out_shape=jax.ShapeDtypeStruct((4, OWN), F32),
+        out_shape=(
+            jax.ShapeDtypeStruct((1, OWN), F32),
+            jax.ShapeDtypeStruct((3, OWN), F32),
+        ),
         in_specs=[vmem, vmem, vmem, vmem, smem, vmem, vmem, vmem, vmem, vmem, vmem, smem],
-        out_specs=vmem,
+        out_specs=(vmem, vmem),
         scratch_shapes=scratch,
         compiler_params=pltpu.CompilerParams(vmem_limit_bytes=60 * 1024 * 1024, **params),
         name="layer",
@@ -727,7 +742,7 @@
         out_weight.reshape(1, -1),
         species_energy,
     )
-    return both[3], both[0:3]
+    return energies.reshape(-1), forces
 
 
 def solution(mesh):

time: 68.1 us -> 67.2 us (0.987)
  Pallas kernels: 64.9 us -> 64 us
    squeeze x1 -> x0, local copies, waits for them, and re-layouts: 1.25 us -> none  [run(): return (both[3], both[0:3])]
    unnamed x3 -> x6, local copies, waits for them, and re-layouts: 0.58 us -> 1.71 us
    pallas_call x1, Pallas kernels: 64.9 us -> 64 us  [run(): pl.pallas_call(functools.partial(body, comm, n_gx, n_gy), out_shape=(jax....]
where the time goes in v5:
time: 67.2 us; the launch traced here: 67 us
  Pallas kernels  64 us (95%)
  local copies, waits for them, and re-layouts  1.71 us (3%)
  between operations  1.31 us (2%)
    pallas_call x1, Pallas kernels, run(): pl.pallas_call(functools.partial(body, comm, n_gx, n_gy), out_shape=(jax....  64 us
    unnamed x6, local copies, waits for them, and re-layouts  1.71 us

profile of v5, /device:TPU:24, one launch (start us, length us, event | category | flops | bytes accessed | tf_op | source)
XLA Modules:
  0.0 67.0 jit_solution(2744879370150861054)
XLA Ops:
  1.3 64.0 %layer.1 = (f32[1,128]{1,0:T(1,128)}, f32[3,128]{1,0:T(4,128)}) custom-call(f32[3,128]{1,0:T(4,128)} %pos_ref.1, bf16[64,128]{1,0:T(8,128)(2,1)} %feat_ref.1, s32[1,128]{1,0:T(1,128)} %bitcast.9, s32[2,3584]{1,0:T(2,128)} %edge_ref.1, s32[1]{0:T(128)S(6)} %copy.16.cnt_ref, s32[1,128]{1,0:T(1,128)} %bitcast.10, s32[1,64]{1,0:T(1,128)} %bitcast.11, ...), custom_call_target="tpu_custom_call" | custom-call | tf_op jit(solution)/shard_map/layer/pallas_call | solution.py:720
  65.3 0.0 copy-start.1
  65.3 0.0 copy-start
  65.3 0.6 copy-done.1
  65.9 0.5 copy.17
  66.4 0.0 copy-done
  66.4 0.6 copy.18
Async XLA Ops:
  65.3 0.6 copy-start.1
  65.3 1.1 %copy-start = (f32[3,128]{1,0:T(4,128)S(1)}, f32[3,128]{1,0:T(4,128)}, u32[]{:S(2)}) copy-start(f32[3,128]{1,0:T(4,128)} %get-tuple-element.9) | copy-start | bytes 4612

commit v6 on v5

--- a/solution.py
+++ b/solution.py
@@ -362,26 +362,36 @@
         sine, sine_last = twice * sine - sine_last, sine
         cosine, cosine_last = twice * cosine - cosine_last, cosine
 
-    def radial_fetch(step):
-        basis = jnp.concatenate([get_eight(bes_d, step), get_eight(slope_d, step)], axis=1)
+    def network_input(basis):
         a, b, c = split3(basis)
         zero = jnp.zeros_like(a)
-        stack = jnp.concatenate([a, b, a, b, c, a, zero, zero], axis=0).astype(BF16)
-        return mm(w6[...], stack)
-
-    def radial_use(step, both):
+        return mm(w6[...], jnp.concatenate([a, b, a, b, c, a, zero, zero], axis=0).astype(BF16))
+
+    def network_output(g):
+        hi, lo = split2(g)
+        return mm(w3[...], jnp.concatenate([hi, lo, hi], axis=0))
+
+    def radial_fetch(step):
+        return network_input(get_eight(bes_d, step))
+
+    def radial_use(step, u):
+        hidden = u / (1.0 + jnp.exp(-u))
+        r_s[:, span(step)] = network_output(get_row(geo_d, 13, step) * hidden)
+
+    ahead(0, STEPS, radial_fetch, radial_use, UNROLL_RADIAL)
+
+    def slope_fetch(step):
+        return network_input(
+            jnp.concatenate([get_eight(bes_d, step), get_eight(slope_d, step)], axis=1)
+        )
+
+    def slope_use(step, both):
         u, u_d = both[:, :TILE], both[:, TILE:]
         gate = 1.0 / (1.0 + jnp.exp(-u))
         hidden = u * gate
         slope = gate + hidden * (1.0 - gate)
         env, env_d = get_row(geo_d, 13, step), get_row(geo_d, 14, step)
-        g = jnp.concatenate([env * hidden, env_d * hidden + env * (slope * u_d)], axis=1)
-        hi, lo = split2(g)
-        radial = mm(w3[...], jnp.concatenate([hi, lo, hi], axis=0))
-        r_s[:, span(step)] = radial[:, :TILE]
-        rp_s[:, span(step)] = radial[:, TILE:]
-
-    ahead(0, STEPS, radial_fetch, radial_use, UNROLL_RADIAL)
+        rp_s[:, span(step)] = network_output(env_d * hidden + env * (slope * u_d))
 
     def messages(target, step, signs, features, degrees):
         radial = r_s[:, span(step)]
@@ -447,14 +457,16 @@
     y_a = push_sums_y(0)
     loop(0, STEPS, other_step_b, UNROLL_SUMS)
     y_b = push_sums_y(1)
-    loop(0, STEPS // 2, own_sum_step, UNROLL_SUMS)
+    loop(0, 3, own_sum_step, UNROLL_SUMS)
     settle(*y_a)
     add_sums_y(0)
     x_a = push_sums_x(0)
-    loop(STEPS // 2, STEPS, own_sum_step, UNROLL_SUMS)
+    loop(3, 8, own_sum_step, UNROLL_SUMS)
     settle(*y_b)
     add_sums_y(1)
     x_b = push_sums_x(1)
+    loop(8, STEPS, own_sum_step, UNROLL_SUMS)
+    ahead(0, STEPS, slope_fetch, slope_use, UNROLL_RADIAL)
 
     def home_sums(group):
         _, start, stop = GROUPS[group]

time: 67.2 us -> 66 us (0.982)
  Pallas kernels: 64 us -> 62.7 us
    pallas_call x1, Pallas kernels: 64 us -> 62.7 us  [run(): pl.pallas_call(functools.partial(body, comm, n_gx, n_gy), out_shape=(jax....]
where the time goes in v6:
time: 66 us; the launch traced here: 65.7 us
  Pallas kernels  62.7 us (95%)
  local copies, waits for them, and re-layouts  1.71 us (3%)
  between operations  1.31 us (2%)
    pallas_call x1, Pallas kernels, run(): pl.pallas_call(functools.partial(body, comm, n_gx, n_gy), out_shape=(jax....  62.7 us
    unnamed x6, local copies, waits for them, and re-layouts  1.71 us

profile of v6, /device:TPU:24, one launch (start us, length us, event | category | flops | bytes accessed | tf_op | source)
XLA Modules:
  0.0 65.7 jit_solution(8450430895932351420)
XLA Ops:
  1.3 62.7 %layer.1 = (f32[1,128]{1,0:T(1,128)}, f32[3,128]{1,0:T(4,128)}) custom-call(f32[3,128]{1,0:T(4,128)} %pos_ref.1, bf16[64,128]{1,0:T(8,128)(2,1)} %feat_ref.1, s32[1,128]{1,0:T(1,128)} %bitcast.9, s32[2,3584]{1,0:T(2,128)} %edge_ref.1, s32[1]{0:T(128)S(6)} %copy.16.cnt_ref, s32[1,128]{1,0:T(1,128)} %bitcast.10, s32[1,64]{1,0:T(1,128)} %bitcast.11, ...), custom_call_target="tpu_custom_call" | custom-call | tf_op jit(solution)/shard_map/layer/pallas_call | solution.py:732
  63.9 0.0 copy-start.1
  64.0 0.0 copy-start
  64.0 0.6 copy-done.1
  64.6 0.5 copy.17
  65.1 0.0 copy-done
  65.1 0.6 copy.18
Async XLA Ops:
  63.9 0.6 copy-start.1
  64.0 1.1 %copy-start = (f32[3,128]{1,0:T(4,128)S(1)}, f32[3,128]{1,0:T(4,128)}, u32[]{:S(2)}) copy-start(f32[3,128]{1,0:T(4,128)} %get-tuple-element.9) | copy-start | bytes 4612
